TPU v7x, 512 devices: a whole 4x4x16 slice. The times are simulated.
512 devices in a mesh: leaf: 64 (over y, z), front: 8 (over x, core).
Axes of the slice: x: 4, y: 4, z: 16, core: 2. Of those that a mesh axis runs over, the one named last changes fastest.
Arguments:
- rhs: float32 [5, 2, 16, 20480], P(None, None, None, ('leaf', 'front')), may hold values from -6 to 6
- inv_blocks: bfloat16 [2, 20480, 19840], P(None, 'leaf', 'front'), may hold values from -1 to 1
- upd_blocks: bfloat16 [2, 20480, 9600], P(None, 'leaf', 'front'), may hold values from -1 to 1
- tile_mask: int32 [64, 30], P('leaf'), may hold values 0 or 1
Outputs:
- solution: float32 [5, 2, 16, 20480], P(None, None, None, ('leaf', 'front'))
All inputs are finite; a program needn't handle non-finite values. No bound on the sum of `tile_mask` on one device may be relied on, other than what follows from the above.
Results may differ from a plain program's by a relative error of at most 0.007.
Values may be sent and summed in bfloat16 or wider, within the bound.
No kernel may reach another device: no remote copies, remote signals or barrier semaphores. Data moves between devices by JAX's collectives and lax.ppermute only.
A program may use at most 64 MiB of HBM per device.

v0:
```python
import jax
import jax.numpy as jnp
from jax import lax
from jax.sharding import PartitionSpec as P


def swapped(value, axis, apart):
    return lax.ppermute(value, axis, [(i, i ^ 1 << apart) for i in range(lax.axis_size(axis))])


def bit_sequence(count):
    return list(range(count))


def subcube_total(partial_value, member_bits):
    position = lax.axis_index("leaf")
    sequence = bit_sequence(member_bits)
    rhs_count, members, rows_dev = partial_value.shape
    summed = partial_value.reshape(rhs_count, members * rows_dev)
    for which_bit in sequence:
        summed = summed + swapped(summed, "leaf", which_bit)
    member = position % members
    return lax.dynamic_slice_in_dim(summed, member * rows_dev, rows_dev, 1)


def complex_product(gathered, real_matrix, imag_matrix):
    rhs_count = gathered.shape[1]
    stacked = gathered.reshape(2 * rhs_count, gathered.shape[2])
    with_real = jnp.dot(stacked, real_matrix, preferred_element_type=jnp.float32)
    with_imag = jnp.dot(stacked, imag_matrix, preferred_element_type=jnp.float32)
    real_part = with_real[:rhs_count] - with_imag[rhs_count:]
    imag_part = with_imag[:rhs_count] + with_real[rhs_count:]
    return jnp.concatenate([real_part, imag_part], axis=0)


def shards(rhs, inv_blocks, upd_blocks, tile_mask):
    blocks = lax.axis_size("leaf")
    levels = blocks.bit_length() - 2
    rows_dev = rhs.shape[3]
    rhs_count = rhs.shape[2]
    full_rows = inv_blocks.shape[1]
    inverse = inv_blocks.reshape(2, full_rows, blocks - 2, rows_dev)
    update = upd_blocks.reshape(2, full_rows, blocks // 2 - 2, rows_dev)
    carried = jnp.zeros((2, rhs_count, rows_dev), jnp.float32)
    solved = []
    for height in range(levels - 1, -1, -1):
        members = blocks >> height + 1
        member_bits = levels - height
        lowered = (rhs[height] - carried).astype(jnp.bfloat16)
        gathered = lax.all_gather(lowered, "front", axis=2, tiled=True)
        offset = blocks - 2 * members
        matrix = inverse[:, :, offset : offset + members, :].reshape(
            2, full_rows, members * rows_dev
        )
        partial_value = complex_product(gathered, matrix[0], matrix[1])
        result = subcube_total(partial_value.reshape(-1, members, rows_dev), member_bits).reshape(
            2, rhs_count, rows_dev
        )
        solved.append(result)
        if height > 0:
            spread = lax.all_gather(result.astype(jnp.bfloat16), "front", axis=2, tiled=True)
            upd_offset = blocks // 2 - 2 * members
            matrix = update[:, :, upd_offset : upd_offset + members, :].reshape(
                2, full_rows, members * rows_dev
            )
            tile_gates = tile_mask[0, upd_offset : upd_offset + members].astype(jnp.float32)
            partial_value = complex_product(spread, matrix[0], matrix[1])
            partial_value = partial_value.reshape(-1, members, rows_dev) * tile_gates[None, :, None]
            carried = subcube_total(partial_value, member_bits).reshape(2, rhs_count, rows_dev)
    return jnp.stack(solved[::-1])


def solution(mesh):
    placed = (
        P(None, None, None, ("leaf", "front")),
        P(None, "leaf", "front"),
        P(None, "leaf", "front"),
        P("leaf", None),
    )
    return jax.shard_map(
        shards,
        mesh=mesh,
        in_specs=placed,
        out_specs=P(None, None, None, ("leaf", "front")),
        check_vma=False,
    )
```

profile of v0, /device:TPU:24, one launch (start us, length us, event | category | flops | bytes accessed | tf_op | source)
XLA Modules:
  0.0 385.5 jit_solution(15044810679732088132)
XLA Ops:
  0.0 6.0 %copy.20 = bf16[2,320,2480]{1,2,0:T(8,128)(2,1)} copy(bf16[2,320,2480]{2,1,0:T(8,128)(2,1)} %param.5) | data formatting | bytes 6348800 | tf_op args[1]
  6.0 0.9 fusion.19
  7.7 13.1 %all-gather = bf16[1,2,16,320]{2,1,0,3:T(2,128)(2,1)S(1)} all-gather(bf16[1,2,16,40]{2,1,0,3:T(2,128)(2,1)S(1)} %copy.38), channel_id=2, replica_groups=mesh['leaf'=64,'front'=8] {'front'}, dimensions={3}, use_global_device_ids=true | all-gather | bytes 23040 | tf_op jit(solution)/shard_map/all_gather | solution.py:50
  21.3 3.8 collective-permute-start
  25.1 1.2 copy.23
  27.1 12.8 %all_gather.28 = bf16[2,16,320]{1,0,2:T(2,128)(2,1)S(1)} all-gather(bf16[2,16,40]{1,0,2:T(2,128)(2,1)S(1)} %copy.21), channel_id=1, replica_groups=mesh['leaf'=64,'front'=8] {'front'}, dimensions={2}, use_global_device_ids=true | all-gather | bytes 23040 | tf_op jit(solution)/shard_map/all_gather | solution.py:61
  40.3 3.8 collective-permute-start.1
  44.1 1.0 fusion.18
  46.8 12.8 %all_gather.29 = bf16[2,16,320]{1,0,2:T(2,128)(2,1)S(1)} all-gather(bf16[2,16,40]{1,0,2:T(2,128)(2,1)S(1)} %copy.24), channel_id=1, replica_groups=mesh['leaf'=64,'front'=8] {'front'}, dimensions={2}, use_global_device_ids=true | all-gather | bytes 23040 | tf_op jit(solution)/shard_map/all_gather | solution.py:50
  60.1 3.8 collective-permute-start.2
  64.0 1.9 collective-permute-done.2
  65.9 5.2 %collective-permute-start.3 = (f32[32,160]{1,0:T(8,128)S(1)}, f32[32,160]{1,0:T(8,128)S(1)}, u32[]{:S(2)}, u32[]{:S(2)}) collective-permute-start(f32[32,160]{1,0:T(8,128)S(1)} %fusion.6), channel_id=1, source_target_pairs={{0,16},{8,24},{16,0},{24,8},{32,48},{40,56},{48,32},{56,40},{64,80... | collective-permute-start | bytes 61448 | tf_op jit(solution)/shard_map/ppermute | solution.py:8
  71.3 1.9 collective-permute-done.3
  73.4 12.8 %all_gather.30 = bf16[2,16,320]{1,0,2:T(2,128)(2,1)S(1)} all-gather(bf16[2,16,40]{1,0,2:T(2,128)(2,1)S(1)} %copy.26), channel_id=1, replica_groups=mesh['leaf'=64,'front'=8] {'front'}, dimensions={2}, use_global_device_ids=true | all-gather | bytes 23040 | tf_op jit(solution)/shard_map/all_gather | solution.py:61
  86.6 3.6 collective-permute-start.4
  90.3 2.2 collective-permute-done.4
  92.5 4.6 %collective-permute-start.5 = (f32[32,160]{1,0:T(8,128)S(1)}, f32[32,160]{1,0:T(8,128)S(1)}, u32[]{:S(2)}, u32[]{:S(2)}) collective-permute-start(f32[32,160]{1,0:T(8,128)S(1)} %add.153), channel_id=1, source_target_pairs={{0,16},{8,24},{16,0},{24,8},{32,48},{40,56},{48,32},{56,40},{64,80... | collective-permute-start | bytes 61448 | tf_op jit(solution)/shard_map/ppermute | solution.py:8
  97.1 1.1 fusion.17
  98.2 1.0 collective-permute-done.5
  99.3 12.8 %all_gather.31 = bf16[2,16,320]{1,0,2:T(2,128)(2,1)S(1)} all-gather(bf16[2,16,40]{1,0,2:T(2,128)(2,1)S(1)} %copy.28), channel_id=1, replica_groups=mesh['leaf'=64,'front'=8] {'front'}, dimensions={2}, use_global_device_ids=true | all-gather | bytes 23040 | tf_op jit(solution)/shard_map/all_gather | solution.py:50
  112.7 3.6 collective-permute-start.6
  116.3 2.4 collective-permute-done.6
  118.7 4.7 %collective-permute-start.7 = (f32[32,320]{1,0:T(8,128)S(1)}, f32[32,320]{1,0:T(8,128)S(1)}, u32[]{:S(2)}, u32[]{:S(2)}) collective-permute-start(f32[32,320]{1,0:T(8,128)S(1)} %fusion.7), channel_id=1, source_target_pairs={{0,16},{8,24},{16,0},{24,8},{32,48},{40,56},{48,32},{56,40},{64,80... | collective-permute-start | bytes 122888 | tf_op jit(solution)/shard_map/ppermute | solution.py:8
  123.4 2.3 collective-permute-done.7
  125.7 9.1 %collective-permute-start.8 = (f32[32,320]{1,0:T(8,128)S(1)}, f32[32,320]{1,0:T(8,128)S(1)}, u32[]{:S(2)}, u32[]{:S(2)}) collective-permute-start(f32[32,320]{1,0:T(8,128)S(1)} %add.157), channel_id=1, source_target_pairs={{0,32},{8,40},{16,48},{24,56},{32,0},{40,8},{48,16},{56,24},{64,96... | collective-permute-start | bytes 122888 | tf_op jit(solution)/shard_map/ppermute | solution.py:8
  135.1 3.9 %collective-permute-done.8 = f32[32,320]{1,0:T(8,128)S(1)} collective-permute-done((f32[32,320]{1,0:T(8,128)S(1)}, f32[32,320]{1,0:T(8,128)S(1)}, u32[]{:S(2)}, u32[]{:S(2)}) %collective-permute-start.8) | collective-permute-done | bytes 40992 | tf_op jit(solution)/shard_map/ppermute | solution.py:8
  139.2 12.8 %all_gather.32 = bf16[2,16,320]{1,0,2:T(2,128)(2,1)S(1)} all-gather(bf16[2,16,40]{1,0,2:T(2,128)(2,1)S(1)} %copy.30), channel_id=1, replica_groups=mesh['leaf'=64,'front'=8] {'front'}, dimensions={2}, use_global_device_ids=true | all-gather | bytes 23040 | tf_op jit(solution)/shard_map/all_gather | solution.py:61
  152.5 1.9 collective-permute-start.9
  154.4 4.1 %collective-permute-done.9 = f32[32,320]{1,0:T(8,128)S(1)} collective-permute-done((f32[32,320]{1,0:T(8,128)S(1)}, f32[32,320]{1,0:T(8,128)S(1)}, u32[]{:S(2)}, u32[]{:S(2)}) %collective-permute-start.9) | collective-permute-done | bytes 40992 | tf_op jit(solution)/shard_map/ppermute | solution.py:8
  158.5 3.0 collective-permute-start.10
  161.4 4.1 %collective-permute-done.10 = f32[32,320]{1,0:T(8,128)S(1)} collective-permute-done((f32[32,320]{1,0:T(8,128)S(1)}, f32[32,320]{1,0:T(8,128)S(1)}, u32[]{:S(2)}, u32[]{:S(2)}) %collective-permute-start.10) | collective-permute-done | bytes 40992 | tf_op jit(solution)/shard_map/ppermute | solution.py:8
  165.5 6.5 %collective-permute-start.11 = (f32[32,320]{1,0:T(8,128)S(1)}, f32[32,320]{1,0:T(8,128)S(1)}, u32[]{:S(2)}, u32[]{:S(2)}) collective-permute-start(f32[32,320]{1,0:T(8,128)S(1)} %add.163), channel_id=1, source_target_pairs={{0,32},{8,40},{16,48},{24,56},{32,0},{40,8},{48,16},{56,24},{64,96... | collective-permute-start | bytes 122888 | tf_op jit(solution)/shard_map/ppermute | solution.py:8
  172.1 1.3 fusion.16
  173.3 3.3 collective-permute-done.11
  176.9 12.8 %all_gather.33 = bf16[2,16,320]{1,0,2:T(2,128)(2,1)S(1)} all-gather(bf16[2,16,40]{1,0,2:T(2,128)(2,1)S(1)} %copy.32), channel_id=1, replica_groups=mesh['leaf'=64,'front'=8] {'front'}, dimensions={2}, use_global_device_ids=true | all-gather | bytes 23040 | tf_op jit(solution)/shard_map/all_gather | solution.py:50
  190.3 1.9 collective-permute-start.12
  192.3 4.7 %collective-permute-done.12 = f32[32,640]{1,0:T(8,128)S(1)} collective-permute-done((f32[32,640]{1,0:T(8,128)S(1)}, f32[32,640]{1,0:T(8,128)S(1)}, u32[]{:S(2)}, u32[]{:S(2)}) %collective-permute-start.12) | collective-permute-done | bytes 81952 | tf_op jit(solution)/shard_map/ppermute | solution.py:8
  196.9 2.6 collective-permute-start.13
  199.5 5.8 %collective-permute-done.13 = f32[32,640]{1,0:T(8,128)S(1)} collective-permute-done((f32[32,640]{1,0:T(8,128)S(1)}, f32[32,640]{1,0:T(8,128)S(1)}, u32[]{:S(2)}, u32[]{:S(2)}) %collective-permute-start.13) | collective-permute-done | bytes 81952 | tf_op jit(solution)/shard_map/ppermute | solution.py:8
  205.3 6.6 %collective-permute-start.14 = (f32[32,640]{1,0:T(8,128)S(1)}, f32[32,640]{1,0:T(8,128)S(1)}, u32[]{:S(2)}, u32[]{:S(2)}) collective-permute-start(f32[32,640]{1,0:T(8,128)S(1)} %add.167), channel_id=1, source_target_pairs={{0,32},{8,40},{16,48},{24,56},{32,0},{40,8},{48,16},{56,24},{64,96... | collective-permute-start | bytes 245768 | tf_op jit(solution)/shard_map/ppermute | solution.py:8
  212.1 7.4 %collective-permute-done.14 = f32[32,640]{1,0:T(8,128)S(1)} collective-permute-done((f32[32,640]{1,0:T(8,128)S(1)}, f32[32,640]{1,0:T(8,128)S(1)}, u32[]{:S(2)}, u32[]{:S(2)}) %collective-permute-start.14) | collective-permute-done | bytes 81952 | tf_op jit(solution)/shard_map/ppermute | solution.py:8
  219.5 9.3 %collective-permute-start.15 = (f32[32,640]{1,0:T(8,128)S(1)}, f32[32,640]{1,0:T(8,128)S(1)}, u32[]{:S(2)}, u32[]{:S(2)}) collective-permute-start(f32[32,640]{1,0:T(8,128)S(1)} %add.168), channel_id=1, source_target_pairs={{0,64},{8,72},{16,80},{24,88},{32,96},{40,104},{48,112},{56,120},{... | collective-permute-start | bytes 245768 | tf_op jit(solution)/shard_map/ppermute | solution.py:8
  229.0 9.9 %collective-permute-done.15 = f32[32,640]{1,0:T(8,128)S(1)} collective-permute-done((f32[32,640]{1,0:T(8,128)S(1)}, f32[32,640]{1,0:T(8,128)S(1)}, u32[]{:S(2)}, u32[]{:S(2)}) %collective-permute-start.15) | collective-permute-done | bytes 81952 | tf_op jit(solution)/shard_map/ppermute | solution.py:8
  239.1 12.8 %all_gather.34 = bf16[2,16,320]{1,0,2:T(2,128)(2,1)S(1)} all-gather(bf16[2,16,40]{1,0,2:T(2,128)(2,1)S(1)} %copy.34), channel_id=1, replica_groups=mesh['leaf'=64,'front'=8] {'front'}, dimensions={2}, use_global_device_ids=true | all-gather | bytes 23040 | tf_op jit(solution)/shard_map/all_gather | solution.py:61
  252.6 1.9 collective-permute-start.16
  254.5 4.7 %collective-permute-done.16 = f32[32,640]{1,0:T(8,128)S(1)} collective-permute-done((f32[32,640]{1,0:T(8,128)S(1)}, f32[32,640]{1,0:T(8,128)S(1)}, u32[]{:S(2)}, u32[]{:S(2)}) %collective-permute-start.16) | collective-permute-done | bytes 81952 | tf_op jit(solution)/shard_map/ppermute | solution.py:8
  259.2 1.9 collective-permute-start.17
  261.1 6.5 %collective-permute-done.17 = f32[32,640]{1,0:T(8,128)S(1)} collective-permute-done((f32[32,640]{1,0:T(8,128)S(1)}, f32[32,640]{1,0:T(8,128)S(1)}, u32[]{:S(2)}, u32[]{:S(2)}) %collective-permute-start.17) | collective-permute-done | bytes 81952 | tf_op jit(solution)/shard_map/ppermute | solution.py:8
  267.5 3.2 collective-permute-start.18
  270.7 9.7 %collective-permute-done.18 = f32[32,640]{1,0:T(8,128)S(1)} collective-permute-done((f32[32,640]{1,0:T(8,128)S(1)}, f32[32,640]{1,0:T(8,128)S(1)}, u32[]{:S(2)}, u32[]{:S(2)}) %collective-permute-start.18) | collective-permute-done | bytes 81952 | tf_op jit(solution)/shard_map/ppermute | solution.py:8
  280.4 7.3 %collective-permute-start.19 = (f32[32,640]{1,0:T(8,128)S(1)}, f32[32,640]{1,0:T(8,128)S(1)}, u32[]{:S(2)}, u32[]{:S(2)}) collective-permute-start(f32[32,640]{1,0:T(8,128)S(1)} %add.175), channel_id=1, source_target_pairs={{0,64},{8,72},{16,80},{24,88},{32,96},{40,104},{48,112},{56,120},{... | collective-permute-start | bytes 245768 | tf_op jit(solution)/shard_map/ppermute | solution.py:8
  287.8 1.7 fusion.15
  289.5 10.0 %collective-permute-done.19 = f32[32,640]{1,0:T(8,128)S(1)} collective-permute-done((f32[32,640]{1,0:T(8,128)S(1)}, f32[32,640]{1,0:T(8,128)S(1)}, u32[]{:S(2)}, u32[]{:S(2)}) %collective-permute-start.19) | collective-permute-done | bytes 81952 | tf_op jit(solution)/shard_map/ppermute | solution.py:8
  299.7 12.8 %all_gather.35 = bf16[2,16,320]{1,0,2:T(2,128)(2,1)S(1)} all-gather(bf16[2,16,40]{1,0,2:T(2,128)(2,1)S(1)} %copy.36), channel_id=1, replica_groups=mesh['leaf'=64,'front'=8] {'front'}, dimensions={2}, use_global_device_ids=true | all-gather | bytes 23040 | tf_op jit(solution)/shard_map/all_gather | solution.py:50
  313.4 1.9 collective-permute-start.20
  315.4 6.4 %collective-permute-done.20 = f32[32,1280]{1,0:T(8,128)S(1)} collective-permute-done((f32[32,1280]{1,0:T(8,128)S(1)}, f32[32,1280]{1,0:T(8,128)S(1)}, u32[]{:S(2)}, u32[]{:S(2)}) %collective-permute-start.20) | collective-permute-done | bytes 163872 | tf_op jit(solution)/shard_map/ppermute | solution.py:8
  321.8 1.9 collective-permute-start.21
  323.7 10.0 %collective-permute-done.21 = f32[32,1280]{1,0:T(8,128)S(1)} collective-permute-done((f32[32,1280]{1,0:T(8,128)S(1)}, f32[32,1280]{1,0:T(8,128)S(1)}, u32[]{:S(2)}, u32[]{:S(2)}) %collective-permute-start.21) | collective-permute-done | bytes 163872 | tf_op jit(solution)/shard_map/ppermute | solution.py:8
  333.7 2.6 collective-permute-start.22
  336.3 16.0 %collective-permute-done.22 = f32[32,1280]{1,0:T(8,128)S(1)} collective-permute-done((f32[32,1280]{1,0:T(8,128)S(1)}, f32[32,1280]{1,0:T(8,128)S(1)}, u32[]{:S(2)}, u32[]{:S(2)}) %collective-permute-start.22) | collective-permute-done | bytes 163872 | tf_op jit(solution)/shard_map/ppermute | solution.py:8
  352.3 7.1 %collective-permute-start.23 = (f32[32,1280]{1,0:T(8,128)S(1)}, f32[32,1280]{1,0:T(8,128)S(1)}, u32[]{:S(2)}, u32[]{:S(2)}) collective-permute-start(f32[32,1280]{1,0:T(8,128)S(1)} %add.180), channel_id=1, source_target_pairs={{0,64},{8,72},{16,80},{24,88},{32,96},{40,104},{48,112},{56,120},{... | collective-permute-start | bytes 491528 | tf_op jit(solution)/shard_map/ppermute | solution.py:8
  359.5 16.6 %collective-permute-done.23 = f32[32,1280]{1,0:T(8,128)S(1)} collective-permute-done((f32[32,1280]{1,0:T(8,128)S(1)}, f32[32,1280]{1,0:T(8,128)S(1)}, u32[]{:S(2)}, u32[]{:S(2)}) %collective-permute-start.23) | collective-permute-done | bytes 163872 | tf_op jit(solution)/shard_map/ppermute | solution.py:8
  376.1 2.7 collective-permute-start.24
  378.8 5.3 %collective-permute-done.24 = f32[32,1280]{1,0:T(8,128)S(1)} collective-permute-done((f32[32,1280]{1,0:T(8,128)S(1)}, f32[32,1280]{1,0:T(8,128)S(1)}, u32[]{:S(2)}, u32[]{:S(2)}) %collective-permute-start.24) | collective-permute-done | bytes 163872 | tf_op jit(solution)/shard_map/ppermute | solution.py:8
  (115 shorter events, 11.7 us)
Async XLA Ops:
  0.0 25.1 %copy-start = (bf16[2,320,1200]{2,1,0:T(8,128)(2,1)S(1)}, bf16[2,320,1200]{2,1,0:T(8,128)(2,1)}, u32[]{:S(2)}) copy-start(bf16[2,320,1200]{2,1,0:T(8,128)(2,1)} %param.6) | copy-start | bytes 4608004
  6.0 20.3 %copy-start.3 = (s32[1,30]{1,0:T(1,128)S(1)}, s32[1,30]{1,0:T(1,128)}, u32[]{:S(2)}) copy-start(s32[1,30]{1,0:T(1,128)} %param.7) | copy-start | bytes 364
  21.3 5.6 %collective-permute-start = (f32[32,80]{1,0:T(8,128)S(1)}, f32[32,80]{1,0:T(8,128)S(1)}, u32[]{:S(2)}, u32[]{:S(2)}) collective-permute-start(f32[32,80]{1,0:T(8,128)S(1)} %pad_maximum_fusion.4), channel_id=1, source_target_pairs={{0,8},{8,0},{16,24},{24,16},{32,40},{40,32},{48,56},{56,48},{64,72... | collective-permute-start | bytes 30728 | tf_op jit(solution)/shard_map/ppermute | solution.py:8
  26.3 72.9 %copy-start.1 = (f32[5,2,16,40]{3,2,1,0:T(8,128)S(1)}, f32[5,2,16,40]{3,2,1,0:T(8,128)}, u32[]{:S(2)}) copy-start(f32[5,2,16,40]{3,2,1,0:T(8,128)} %param.4) | copy-start | bytes 76804
  40.3 5.6 %collective-permute-start.1 = (f32[32,80]{1,0:T(8,128)S(1)}, f32[32,80]{1,0:T(8,128)S(1)}, u32[]{:S(2)}, u32[]{:S(2)}) collective-permute-start(f32[32,80]{1,0:T(8,128)S(1)} %maximum_multiply_fusion.3), channel_id=1, source_target_pairs={{0,8},{8,0},{16,24},{24,16},{32,40},{40,32},{48,56},{56,48},{64,72... | collective-permute-start | bytes 30728 | tf_op jit(solution)/shard_map/ppermute | solution.py:8
  60.1 5.8 %collective-permute-start.2 = (f32[32,160]{1,0:T(8,128)S(1)}, f32[32,160]{1,0:T(8,128)S(1)}, u32[]{:S(2)}, u32[]{:S(2)}) collective-permute-start(f32[32,160]{1,0:T(8,128)S(1)} %pad_maximum_fusion.3), channel_id=1, source_target_pairs={{0,8},{8,0},{16,24},{24,16},{32,40},{40,32},{48,56},{56,48},{64,72... | collective-permute-start | bytes 61448 | tf_op jit(solution)/shard_map/ppermute | solution.py:8
  65.9 7.3 %collective-permute-start.3 = (f32[32,160]{1,0:T(8,128)S(1)}, f32[32,160]{1,0:T(8,128)S(1)}, u32[]{:S(2)}, u32[]{:S(2)}) collective-permute-start(f32[32,160]{1,0:T(8,128)S(1)} %fusion.6), channel_id=1, source_target_pairs={{0,16},{8,24},{16,0},{24,8},{32,48},{40,56},{48,32},{56,40},{64,80... | collective-permute-start | bytes 61448 | tf_op jit(solution)/shard_map/ppermute | solution.py:8
  86.6 5.8 %collective-permute-start.4 = (f32[32,160]{1,0:T(8,128)S(1)}, f32[32,160]{1,0:T(8,128)S(1)}, u32[]{:S(2)}, u32[]{:S(2)}) collective-permute-start(f32[32,160]{1,0:T(8,128)S(1)} %maximum_multiply_fusion.2), channel_id=1, source_target_pairs={{0,8},{8,0},{16,24},{24,16},{32,40},{40,32},{48,56},{56,48},{64,72... | collective-permute-start | bytes 61448 | tf_op jit(solution)/shard_map/ppermute | solution.py:8
  92.5 6.7 %collective-permute-start.5 = (f32[32,160]{1,0:T(8,128)S(1)}, f32[32,160]{1,0:T(8,128)S(1)}, u32[]{:S(2)}, u32[]{:S(2)}) collective-permute-start(f32[32,160]{1,0:T(8,128)S(1)} %add.153), channel_id=1, source_target_pairs={{0,16},{8,24},{16,0},{24,8},{32,48},{40,56},{48,32},{56,40},{64,80... | collective-permute-start | bytes 61448 | tf_op jit(solution)/shard_map/ppermute | solution.py:8
  112.7 6.0 %collective-permute-start.6 = (f32[32,320]{1,0:T(8,128)S(1)}, f32[32,320]{1,0:T(8,128)S(1)}, u32[]{:S(2)}, u32[]{:S(2)}) collective-permute-start(f32[32,320]{1,0:T(8,128)S(1)} %pad_maximum_fusion.2), channel_id=1, source_target_pairs={{0,8},{8,0},{16,24},{24,16},{32,40},{40,32},{48,56},{56,48},{64,72... | collective-permute-start | bytes 122888 | tf_op jit(solution)/shard_map/ppermute | solution.py:8
  118.7 7.1 %collective-permute-start.7 = (f32[32,320]{1,0:T(8,128)S(1)}, f32[32,320]{1,0:T(8,128)S(1)}, u32[]{:S(2)}, u32[]{:S(2)}) collective-permute-start(f32[32,320]{1,0:T(8,128)S(1)} %fusion.7), channel_id=1, source_target_pairs={{0,16},{8,24},{16,0},{24,8},{32,48},{40,56},{48,32},{56,40},{64,80... | collective-permute-start | bytes 122888 | tf_op jit(solution)/shard_map/ppermute | solution.py:8
  125.7 13.2 %collective-permute-start.8 = (f32[32,320]{1,0:T(8,128)S(1)}, f32[32,320]{1,0:T(8,128)S(1)}, u32[]{:S(2)}, u32[]{:S(2)}) collective-permute-start(f32[32,320]{1,0:T(8,128)S(1)} %add.157), channel_id=1, source_target_pairs={{0,32},{8,40},{16,48},{24,56},{32,0},{40,8},{48,16},{56,24},{64,96... | collective-permute-start | bytes 122888 | tf_op jit(solution)/shard_map/ppermute | solution.py:8
  152.5 6.0 %collective-permute-start.9 = (f32[32,320]{1,0:T(8,128)S(1)}, f32[32,320]{1,0:T(8,128)S(1)}, u32[]{:S(2)}, u32[]{:S(2)}) collective-permute-start(f32[32,320]{1,0:T(8,128)S(1)} %maximum_multiply_fusion.1), channel_id=1, source_target_pairs={{0,8},{8,0},{16,24},{24,16},{32,40},{40,32},{48,56},{56,48},{64,72... | collective-permute-start | bytes 122888 | tf_op jit(solution)/shard_map/ppermute | solution.py:8
  158.5 7.0 %collective-permute-start.10 = (f32[32,320]{1,0:T(8,128)S(1)}, f32[32,320]{1,0:T(8,128)S(1)}, u32[]{:S(2)}, u32[]{:S(2)}) collective-permute-start(f32[32,320]{1,0:T(8,128)S(1)} %add.162), channel_id=1, source_target_pairs={{0,16},{8,24},{16,0},{24,8},{32,48},{40,56},{48,32},{56,40},{64,80... | collective-permute-start | bytes 122888 | tf_op jit(solution)/shard_map/ppermute | solution.py:8
  165.5 11.2 %collective-permute-start.11 = (f32[32,320]{1,0:T(8,128)S(1)}, f32[32,320]{1,0:T(8,128)S(1)}, u32[]{:S(2)}, u32[]{:S(2)}) collective-permute-start(f32[32,320]{1,0:T(8,128)S(1)} %add.163), channel_id=1, source_target_pairs={{0,32},{8,40},{16,48},{24,56},{32,0},{40,8},{48,16},{56,24},{64,96... | collective-permute-start | bytes 122888 | tf_op jit(solution)/shard_map/ppermute | solution.py:8
  190.3 6.6 %collective-permute-start.12 = (f32[32,640]{1,0:T(8,128)S(1)}, f32[32,640]{1,0:T(8,128)S(1)}, u32[]{:S(2)}, u32[]{:S(2)}) collective-permute-start(f32[32,640]{1,0:T(8,128)S(1)} %pad_maximum_fusion.1), channel_id=1, source_target_pairs={{0,8},{8,0},{16,24},{24,16},{32,40},{40,32},{48,56},{56,48},{64,72... | collective-permute-start | bytes 245768 | tf_op jit(solution)/shard_map/ppermute | solution.py:8
  196.9 8.4 %collective-permute-start.13 = (f32[32,640]{1,0:T(8,128)S(1)}, f32[32,640]{1,0:T(8,128)S(1)}, u32[]{:S(2)}, u32[]{:S(2)}) collective-permute-start(f32[32,640]{1,0:T(8,128)S(1)} %fusion.8), channel_id=1, source_target_pairs={{0,16},{8,24},{16,0},{24,8},{32,48},{40,56},{48,32},{56,40},{64,80... | collective-permute-start | bytes 245768 | tf_op jit(solution)/shard_map/ppermute | solution.py:8
  205.3 14.2 %collective-permute-start.14 = (f32[32,640]{1,0:T(8,128)S(1)}, f32[32,640]{1,0:T(8,128)S(1)}, u32[]{:S(2)}, u32[]{:S(2)}) collective-permute-start(f32[32,640]{1,0:T(8,128)S(1)} %add.167), channel_id=1, source_target_pairs={{0,32},{8,40},{16,48},{24,56},{32,0},{40,8},{48,16},{56,24},{64,96... | collective-permute-start | bytes 245768 | tf_op jit(solution)/shard_map/ppermute | solution.py:8
  219.5 19.4 %collective-permute-start.15 = (f32[32,640]{1,0:T(8,128)S(1)}, f32[32,640]{1,0:T(8,128)S(1)}, u32[]{:S(2)}, u32[]{:S(2)}) collective-permute-start(f32[32,640]{1,0:T(8,128)S(1)} %add.168), channel_id=1, source_target_pairs={{0,64},{8,72},{16,80},{24,88},{32,96},{40,104},{48,112},{56,120},{... | collective-permute-start | bytes 245768 | tf_op jit(solution)/shard_map/ppermute | solution.py:8
  252.6 6.6 %collective-permute-start.16 = (f32[32,640]{1,0:T(8,128)S(1)}, f32[32,640]{1,0:T(8,128)S(1)}, u32[]{:S(2)}, u32[]{:S(2)}) collective-permute-start(f32[32,640]{1,0:T(8,128)S(1)} %maximum_multiply_fusion), channel_id=1, source_target_pairs={{0,8},{8,0},{16,24},{24,16},{32,40},{40,32},{48,56},{56,48},{64,72... | collective-permute-start | bytes 245768 | tf_op jit(solution)/shard_map/ppermute | solution.py:8
  259.2 8.4 %collective-permute-start.17 = (f32[32,640]{1,0:T(8,128)S(1)}, f32[32,640]{1,0:T(8,128)S(1)}, u32[]{:S(2)}, u32[]{:S(2)}) collective-permute-start(f32[32,640]{1,0:T(8,128)S(1)} %add.173), channel_id=1, source_target_pairs={{0,16},{8,24},{16,0},{24,8},{32,48},{40,56},{48,32},{56,40},{64,80... | collective-permute-start | bytes 245768 | tf_op jit(solution)/shard_map/ppermute | solution.py:8
  267.5 12.9 %collective-permute-start.18 = (f32[32,640]{1,0:T(8,128)S(1)}, f32[32,640]{1,0:T(8,128)S(1)}, u32[]{:S(2)}, u32[]{:S(2)}) collective-permute-start(f32[32,640]{1,0:T(8,128)S(1)} %add.174), channel_id=1, source_target_pairs={{0,32},{8,40},{16,48},{24,56},{32,0},{40,8},{48,16},{56,24},{64,96... | collective-permute-start | bytes 245768 | tf_op jit(solution)/shard_map/ppermute | solution.py:8
  280.4 19.0 %collective-permute-start.19 = (f32[32,640]{1,0:T(8,128)S(1)}, f32[32,640]{1,0:T(8,128)S(1)}, u32[]{:S(2)}, u32[]{:S(2)}) collective-permute-start(f32[32,640]{1,0:T(8,128)S(1)} %add.175), channel_id=1, source_target_pairs={{0,64},{8,72},{16,80},{24,88},{32,96},{40,104},{48,112},{56,120},{... | collective-permute-start | bytes 245768 | tf_op jit(solution)/shard_map/ppermute | solution.py:8
  313.4 8.3 %collective-permute-start.20 = (f32[32,1280]{1,0:T(8,128)S(1)}, f32[32,1280]{1,0:T(8,128)S(1)}, u32[]{:S(2)}, u32[]{:S(2)}) collective-permute-start(f32[32,1280]{1,0:T(8,128)S(1)} %pad_maximum_fusion), channel_id=1, source_target_pairs={{0,8},{8,0},{16,24},{24,16},{32,40},{40,32},{48,56},{56,48},{64,72... | collective-permute-start | bytes 491528 | tf_op jit(solution)/shard_map/ppermute | solution.py:8
  321.8 11.9 %collective-permute-start.21 = (f32[32,1280]{1,0:T(8,128)S(1)}, f32[32,1280]{1,0:T(8,128)S(1)}, u32[]{:S(2)}, u32[]{:S(2)}) collective-permute-start(f32[32,1280]{1,0:T(8,128)S(1)} %fusion.9), channel_id=1, source_target_pairs={{0,16},{8,24},{16,0},{24,8},{32,48},{40,56},{48,32},{56,40},{64,80... | collective-permute-start | bytes 491528 | tf_op jit(solution)/shard_map/ppermute | solution.py:8
  333.7 18.6 %collective-permute-start.22 = (f32[32,1280]{1,0:T(8,128)S(1)}, f32[32,1280]{1,0:T(8,128)S(1)}, u32[]{:S(2)}, u32[]{:S(2)}) collective-permute-start(f32[32,1280]{1,0:T(8,128)S(1)} %add.179), channel_id=1, source_target_pairs={{0,32},{8,40},{16,48},{24,56},{32,0},{40,8},{48,16},{56,24},{64,96... | collective-permute-start | bytes 491528 | tf_op jit(solution)/shard_map/ppermute | solution.py:8
  352.3 23.7 %collective-permute-start.23 = (f32[32,1280]{1,0:T(8,128)S(1)}, f32[32,1280]{1,0:T(8,128)S(1)}, u32[]{:S(2)}, u32[]{:S(2)}) collective-permute-start(f32[32,1280]{1,0:T(8,128)S(1)} %add.180), channel_id=1, source_target_pairs={{0,64},{8,72},{16,80},{24,88},{32,96},{40,104},{48,112},{56,120},{... | collective-permute-start | bytes 491528 | tf_op jit(solution)/shard_map/ppermute | solution.py:8
  376.1 8.0 %collective-permute-start.24 = (f32[32,1280]{1,0:T(8,128)S(1)}, f32[32,1280]{1,0:T(8,128)S(1)}, u32[]{:S(2)}, u32[]{:S(2)}) collective-permute-start(f32[32,1280]{1,0:T(8,128)S(1)} %add.181), channel_id=1, source_target_pairs={{0,128},{8,136},{16,144},{24,152},{32,160},{40,168},{48,176},{56,1... | collective-permute-start | bytes 491528 | tf_op jit(solution)/shard_map/ppermute | solution.py:8
  384.2 0.6 copy-start.2
where the time goes:
time: 387 us; the launch traced here: 385 us
  waiting for transfers between devices  141 us (36%)
  blocking collectives  115 us (30%)
  starting transfers between devices  105 us (27%)
  local copies, waits for them, and re-layouts  17.8 us (5%)
  matrix products  3.9 us (1%)
    ppermute x25, waiting for transfers between devices, swapped(): lax.ppermute(value, axis, [(i, i ^ 1 << apart) for i in range(lax.axis_si...  141 us
    ppermute x25, starting transfers between devices, swapped(): lax.ppermute(value, axis, [(i, i ^ 1 << apart) for i in range(lax.axis_si...  105 us
    all_gather x5, blocking collectives, shards(): gathered = lax.all_gather(lowered, 'front', axis=2, tiled=True)  64.2 us
    all_gather x4, blocking collectives, shards(): lax.all_gather(result.astype(jnp.bfloat16), 'front', axis=2, tiled=True)  51.1 us
    unnamed x15, local copies, waits for them, and re-layouts  7.93 us
  transfers between devices with their start and end apart: 25, of which 25 were waited for; matrix products, arithmetic and copies ran while one was open for 2% of the time, Pallas kernels for 0%

commit v1 on v0

v1 whole, which is shorter than its diff:
```python
import jax
import jax.numpy as jnp
from jax import lax
from jax.experimental import pallas as pl
from jax.experimental.pallas import tpu as pltpu
from jax.sharding import Mesh
from jax.sharding import PartitionSpec as P

LEAF = ("y1", "y0", "z3", "z2", "z1", "z0")
FRONT = ("x", "core")
SPLIT = (1,)


def lane_window(columns, start, width):
    first = start // 128 * 128
    last = min(-(-(start + width) // 128) * 128, columns)
    return first, last


def whole(space=pltpu.VMEM):
    return pl.BlockSpec(memory_space=space)


def call(body, outs, inputs, scalars=0):
    specs = [whole(pltpu.SMEM)] * scalars + [whole()] * (len(inputs) - scalars)
    return pl.pallas_call(
        body,
        out_shape=outs,
        in_specs=specs,
        out_specs=jax.tree.map(lambda _: whole(), outs),
    )(*inputs)


def message(real, imag):
    return jnp.concatenate([real, imag], axis=1)


def summed_chunks(received, fronts):
    count, rows, lanes = received.shape
    parts = received[...].astype(jnp.float32).reshape(count // fronts, fronts, rows, lanes)
    return jnp.sum(parts, axis=0)


def own_chunk(chunks, own):
    total = jnp.zeros(chunks.shape[1:], jnp.float32)
    for c in range(chunks.shape[0]):
        total = total + jnp.where(own == c, chunks[c], 0.0)
    return total


def stacked_input(chunks):
    half = chunks.shape[2] // 2
    real = jnp.concatenate([c[:, :half] for c in chunks], axis=1)
    imag = jnp.concatenate([c[:, half:] for c in chunks], axis=1)
    upper = jnp.concatenate([real, -imag], axis=1)
    lower = jnp.concatenate([imag, real], axis=1)
    return jnp.concatenate([upper, lower], axis=0).astype(jnp.bfloat16)


def products(chunks, matrix, start, width):
    first, last = lane_window(matrix.shape[2], start, width)
    weights = matrix[:, :, first:last].reshape(-1, last - first)
    out = jnp.dot(stacked_input(chunks), weights, preferred_element_type=jnp.float32)
    return out, start - first


def member_message(out, shift, member, rows_dev):
    rhs_count = out.shape[0] // 2
    lane = shift + member * rows_dev
    piece = out[:, lane : lane + rows_dev]
    return message(piece[:rhs_count], piece[rhs_count:])


def put(sent, member, value, copies):
    value = value.astype(jnp.bfloat16)
    for c in range(copies):
        sent[member * copies + c] = value


def shards(rhs, inv_blocks, upd_blocks, tile_mask):
    axes = {name: lax.axis_size(name) for name in LEAF + FRONT}
    fronts = axes["x"] * axes["core"]
    blocks = 1
    for name in LEAF:
        blocks *= axes[name]
    levels, _, rhs_count, rows_dev = rhs.shape
    msg = (rhs_count, 2 * rows_dev)
    leaf = lax.axis_index(LEAF).astype(jnp.int32)
    front = lax.axis_index(FRONT).astype(jnp.int32)
    place = jnp.stack([leaf, front])
    bf16 = jnp.bfloat16

    def sent_shape(count):
        return jax.ShapeDtypeStruct((count,) + msg, bf16)

    sol_shape = jax.ShapeDtypeStruct((2, rhs_count, rows_dev), jnp.float32)

    def write_solution(sol, value):
        sol[0] = value[:, :rows_dev]
        sol[1] = value[:, rows_dev:]

    def over(value, names):
        return lax.all_to_all(value, names, 0, 0, tiled=True)

    def first_body(rhs_ref, sent):
        put(sent, 0, message(rhs_ref[levels - 1, 0], rhs_ref[levels - 1, 1]), fronts)

    def invert(level, received):
        members = blocks >> (level + 1)
        copies = 1 if level in SPLIT or level == 0 else fronts

        def body(received_ref, matrix, sent):
            chunks = summed_chunks(received_ref, fronts)
            out, shift = products(chunks, matrix, (blocks - 2 * members) * rows_dev, members * rows_dev)
            for a in range(members):
                put(sent, a, member_message(out, shift, a, rows_dev), copies)

        return call(body, sent_shape(members * copies), (received, inv_blocks))

    def update(level, received, known):
        members = blocks >> (level + 1)
        copies = 1 if level in SPLIT else fronts
        offset = blocks // 2 - 2 * members

        def body(place_ref, mask, received_ref, rhs_ref, matrix, *outs):
            sent = outs[0]
            chunks = summed_chunks(received_ref, fronts)
            if not known:
                write_solution(outs[1], own_chunk(chunks, place_ref[1]))
            out, shift = products(chunks, matrix, offset * rows_dev, members * rows_dev)
            own = place_ref[0] % members
            right = message(rhs_ref[level - 1, 0], rhs_ref[level - 1, 1])
            for a in range(members):
                gate = mask[0, offset + a].astype(jnp.float32)
                part = member_message(out, shift, a, rows_dev) * gate
                put(sent, a, jnp.where(own == a, right, 0.0) - part, copies)

        outs = (sent_shape(members * copies),) + (() if known else (sol_shape,))
        return call(body, outs, (place, tile_mask, received, rhs, upd_blocks), 2)

    def combine(received, solution):
        def body(received_ref, sent, *outs):
            total = summed_chunks(received_ref, 1)[0]
            if solution:
                write_solution(outs[0], total)
            put(sent, 0, total, fronts)

        outs = (sent_shape(fronts),) + ((sol_shape,) if solution else ())
        return call(body, outs, (received,))

    def finish(received, solved):
        def body(received_ref, *refs):
            out = refs[-1]
            write_solution(out.at[0], summed_chunks(received_ref, 1)[0])
            for level in range(1, levels):
                out[level] = refs[level - 1][...]

        return call(body, jax.ShapeDtypeStruct(rhs.shape, jnp.float32), (received, *solved))

    received = over(call(first_body, sent_shape(fronts), (rhs,)), FRONT)
    solved = [None] * levels
    for level in range(levels - 1, -1, -1):
        group = LEAF[len(LEAF) - (levels - level) :]
        sent = invert(level, received)
        if level == 0:
            return finish(over(sent, group), solved[1:])
        if level in SPLIT:
            sent, solved[level] = combine(over(sent, group), True)
            (sent,) = update(level, over(sent, FRONT), True)
            (sent,) = combine(over(sent, group), False)
            received = over(sent, FRONT)
        else:
            sent, solved[level] = update(level, over(sent, group + FRONT), False)
            received = over(sent, group + FRONT)


def solution(mesh):
    finer = Mesh(mesh.devices.reshape(2, 2, 2, 2, 2, 2, 4, 2), LEAF + FRONT)
    placed = (
        P(None, None, None, LEAF + FRONT),
        P(None, LEAF, FRONT),
        P(None, LEAF, FRONT),
        P(LEAF, None),
    )
    return jax.shard_map(
        shards,
        mesh=finer,
        in_specs=placed,
        out_specs=P(None, None, None, LEAF + FRONT),
        check_vma=False,
    )
```

time: 387 us -> 228 us (0.59)
  waiting for transfers between devices: 141 us -> 5.53 us
  starting transfers between devices: 105 us -> 3.9 us
  blocking collectives: 115 us -> 183 us
  Pallas kernels: 0 us -> 32.1 us
  local copies, waits for them, and re-layouts: 17.8 us -> 0.63 us
  matrix products: 3.9 us -> 0 us
    all_to_all x0 -> x11, blocking collectives: none -> 183 us  [over(): return lax.all_to_all(value, names, 0, 0, tiled=True)]
    ppermute x25 -> x0, waiting for transfers between devices: 141 us -> none  [swapped(): lax.ppermute(value, axis, [(i, i ^ 1 << apart) for i in range(lax.axis_si...]
    all_gather x9 -> x0, blocking collectives: 115 us -> none  [the longest x5 64.2 us: shards(): gathered = lax.all_gather(lowered, 'front', axis=2, tiled=True)]
    ppermute x25 -> x0, starting transfers between devices: 105 us -> none  [swapped(): lax.ppermute(value, axis, [(i, i ^ 1 << apart) for i in range(lax.axis_si...]
    pallas_call x0 -> x13, Pallas kernels: none -> 32.1 us  [call(): pl.pallas_call(body, out_shape=outs, in_specs=specs, out_specs=jax.tree.m...]
    unnamed x15 -> x2, local copies, waits for them, and re-layouts: 7.93 us -> 0.63 us
    slice x10 -> x0, local copies, waits for them, and re-layouts: 6.88 us -> none  [the longest x5 5.96 us: shards(): partial_value = complex_product(gathered, matrix[0], matrix[1])]
    all_to_all x0 -> x1, waiting for transfers between devices: none -> 5.53 us  [over(): return lax.all_to_all(value, names, 0, 0, tiled=True)]
  transfers between devices with their start and end apart: 25 -> 1, of which waited for: 25 -> 1; matrix products, arithmetic and copies ran while one was open for 2% -> 0% of each run, Pallas kernels for 0% -> 0%
where the time goes in v1:
time: 228 us; the launch traced here: 225 us
  blocking collectives  183 us (80%)
  Pallas kernels  32.1 us (14%)
  waiting for transfers between devices  5.53 us (2%)
  starting transfers between devices  3.9 us (2%)
    all_to_all x11, blocking collectives, over(): return lax.all_to_all(value, names, 0, 0, tiled=True)  183 us
    pallas_call x13, Pallas kernels, call(): pl.pallas_call(body, out_shape=outs, in_specs=specs, out_specs=jax.tree.m...  32.1 us
    all_to_all x1, waiting for transfers between devices, over(): return lax.all_to_all(value, names, 0, 0, tiled=True)  5.53 us
  transfers between devices with their start and end apart: 1, of which 1 were waited for; matrix products, arithmetic and copies ran while one was open for 0% of the time, Pallas kernels for 0%

profile of v1, /device:TPU:24, one launch (start us, length us, event | category | flops | bytes accessed | tf_op | source)
XLA Modules:
  0.0 225.5 jit_solution(9994104122078417847)
XLA Ops:
  0.0 1.6 shard_map.46
  1.6 9.8 %all_to_all.60.received_ref = bf16[8,16,80]{2,1,0:T(8,128)(2,1)} all-to-all(bf16[8,16,80]{2,1,0:T(8,128)(2,1)} %shard_map.46), channel_id=1, replica_groups=mesh['y1'=2,'y0'=2,'z3'=2,'z2'=2,'z1'=2,'z0'=2,'x'=4,'core'=2] {'x','core'}, dimensions={0} | all-to-all | bytes 40960 | tf_op jit(solution)/shard_map/all_to_all | solution.py:103
  11.4 2.9 %shard_map.47 = bf16[16,16,80]{2,1,0:T(8,128)(2,1)} custom-call(bf16[8,16,80]{2,1,0:T(8,128)(2,1)} %all_to_all.60.received_ref, bf16[2,320,2480]{2,1,0:T(8,128)(2,1)} %matrix.17), custom_call_target="tpu_custom_call" | custom-call | tf_op jit(solution)/shard_map/pallas_call | solution.py:26
  14.4 3.9 %all-to-all-start.1 = ((bf16[16,16,80]{2,1,0:T(8,128)(2,1)}), bf16[16,16,80]{2,1,0:T(8,128)(2,1)S(1)}, u32[]{:S(2)}, u32[]{:S(2)}) async-start(bf16[16,16,80]{2,1,0:T(8,128)(2,1)} %shard_map.47), calls=%async_computation.1 | async-start | bytes 131072 | tf_op jit(solution)/shard_map/all_to_all | solution.py:103
  18.3 0.6 pad_add_fusion.place_ref
  18.9 5.5 %all-to-all-done.1.received_ref = bf16[16,16,80]{2,1,0:T(8,128)(2,1)S(1)} async-done(((bf16[16,16,80]{2,1,0:T(8,128)(2,1)}), bf16[16,16,80]{2,1,0:T(8,128)(2,1)S(1)}, u32[]{:S(2)}, u32[]{:S(2)}) %all-to-all-start.1) | async-done | bytes 40992 | tf_op jit(solution)/shard_map/all_to_all | solution.py:103
  24.4 0.0 copy-start
  24.4 0.6 copy-done
  25.1 2.5 %shard_map.48 = (bf16[16,16,80]{2,1,0:T(8,128)(2,1)}, f32[2,16,40]{2,1,0:T(8,128)}) custom-call(s32[2]{0:T(128)} %pad_add_fusion.place_ref, s32[1,30]{1,0:T(1,128)} %mask.7, bf16[16,16,80]{2,1,0:T(8,128)(2,1)} %copy-done, f32[5,2,16,40]{3,2,1,0:T(8,128)} %rhs_ref.9, bf16[2,320,1200]{2,1,0:T(8,128)(2,1)} %matrix.16), custom_call_target="tpu_custom_call" | custom-call | tf_op jit(solution)/shard_map/pallas_call | solution.py:26
  27.6 10.3 %all_to_all.61.received_ref = bf16[16,16,80]{2,1,0:T(8,128)(2,1)} all-to-all(bf16[16,16,80]{2,1,0:T(8,128)(2,1)} %get-tuple-element.13), channel_id=1, replica_groups=mesh['y1'=2,'y0'=2,'z3'=2,'z2'=2,'z1'=2,'z0'=2,'x'=4,'core'=2] {'z0','x'..., dimensions={0} | all-to-all | bytes 81920 | tf_op jit(solution)/shard_map/all_to_all | solution.py:103
  37.9 3.0 %shard_map.49 = bf16[32,16,80]{2,1,0:T(8,128)(2,1)} custom-call(bf16[16,16,80]{2,1,0:T(8,128)(2,1)} %all_to_all.61.received_ref, bf16[2,320,2480]{2,1,0:T(8,128)(2,1)} %matrix.17), custom_call_target="tpu_custom_call" | custom-call | tf_op jit(solution)/shard_map/pallas_call | solution.py:26
  40.9 14.3 %all_to_all.62.received_ref = bf16[32,16,80]{2,1,0:T(8,128)(2,1)} all-to-all(bf16[32,16,80]{2,1,0:T(8,128)(2,1)} %shard_map.49), channel_id=1, replica_groups=mesh['y1'=2,'y0'=2,'z3'=2,'z2'=2,'z1'=2,'z0'=2,'x'=4,'core'=2] {'z1','z0..., dimensions={0} | all-to-all | bytes 163840 | tf_op jit(solution)/shard_map/all_to_all | solution.py:103
  55.2 2.6 %shard_map.50 = (bf16[32,16,80]{2,1,0:T(8,128)(2,1)}, f32[2,16,40]{2,1,0:T(8,128)}) custom-call(s32[2]{0:T(128)} %pad_add_fusion.place_ref, s32[1,30]{1,0:T(1,128)} %mask.7, bf16[32,16,80]{2,1,0:T(8,128)(2,1)} %all_to_all.62.received_ref, f32[5,2,16,40]{3,2,1,0:T(8,128)} %rhs_ref.9, bf16[2,320,1200]{2,1,0:T(8,128)(2,1)} %matrix.16), custom_call_target="tpu_custom_call" | custom-call | tf_op jit(solution)/shard_map/pallas_call | solution.py:26
  57.8 13.1 %all_to_all.63.received_ref = bf16[32,16,80]{2,1,0:T(8,128)(2,1)} all-to-all(bf16[32,16,80]{2,1,0:T(8,128)(2,1)} %get-tuple-element.14), channel_id=1, replica_groups=mesh['y1'=2,'y0'=2,'z3'=2,'z2'=2,'z1'=2,'z0'=2,'x'=4,'core'=2] {'z1','z0..., dimensions={0} | all-to-all | bytes 163840 | tf_op jit(solution)/shard_map/all_to_all | solution.py:103
  70.9 3.1 %shard_map.51 = bf16[64,16,80]{2,1,0:T(8,128)(2,1)} custom-call(bf16[32,16,80]{2,1,0:T(8,128)(2,1)} %all_to_all.63.received_ref, bf16[2,320,2480]{2,1,0:T(8,128)(2,1)} %matrix.17), custom_call_target="tpu_custom_call" | custom-call | tf_op jit(solution)/shard_map/pallas_call | solution.py:26
  74.1 30.7 %all_to_all.64.received_ref = bf16[64,16,80]{2,1,0:T(8,128)(2,1)} all-to-all(bf16[64,16,80]{2,1,0:T(8,128)(2,1)} %shard_map.51), channel_id=1, replica_groups=mesh['y1'=2,'y0'=2,'z3'=2,'z2'=2,'z1'=2,'z0'=2,'x'=4,'core'=2] {'z2','z1..., dimensions={0} | all-to-all | bytes 327680 | tf_op jit(solution)/shard_map/all_to_all | solution.py:103
  104.8 2.7 %shard_map.52 = (bf16[64,16,80]{2,1,0:T(8,128)(2,1)}, f32[2,16,40]{2,1,0:T(8,128)}) custom-call(s32[2]{0:T(128)} %pad_add_fusion.place_ref, s32[1,30]{1,0:T(1,128)} %mask.7, bf16[64,16,80]{2,1,0:T(8,128)(2,1)} %all_to_all.64.received_ref, f32[5,2,16,40]{3,2,1,0:T(8,128)} %rhs_ref.9, bf16[2,320,1200]{2,1,0:T(8,128)(2,1)} %matrix.16), custom_call_target="tpu_custom_call" | custom-call | tf_op jit(solution)/shard_map/pallas_call | solution.py:26
  107.5 25.9 %all_to_all.65.received_ref = bf16[64,16,80]{2,1,0:T(8,128)(2,1)} all-to-all(bf16[64,16,80]{2,1,0:T(8,128)(2,1)} %get-tuple-element.15), channel_id=1, replica_groups=mesh['y1'=2,'y0'=2,'z3'=2,'z2'=2,'z1'=2,'z0'=2,'x'=4,'core'=2] {'z2','z1..., dimensions={0} | all-to-all | bytes 327680 | tf_op jit(solution)/shard_map/all_to_all | solution.py:103
  133.4 3.1 %shard_map.53 = bf16[16,16,80]{2,1,0:T(8,128)(2,1)} custom-call(bf16[64,16,80]{2,1,0:T(8,128)(2,1)} %all_to_all.65.received_ref, bf16[2,320,2480]{2,1,0:T(8,128)(2,1)} %matrix.17), custom_call_target="tpu_custom_call" | custom-call | tf_op jit(solution)/shard_map/pallas_call | solution.py:26
  136.5 22.0 %all_to_all.66.received_ref = bf16[16,16,80]{2,1,0:T(8,128)(2,1)} all-to-all(bf16[16,16,80]{2,1,0:T(8,128)(2,1)} %shard_map.53), channel_id=1, replica_groups=mesh['y1'=2,'y0'=2,'z3'=2,'z2'=2,'z1'=2,'z0'=2,'x'=4,'core'=2] {'z3','z2..., dimensions={0} | all-to-all | bytes 81920 | tf_op jit(solution)/shard_map/all_to_all | solution.py:103
  158.5 1.5 shard_map.54
  160.0 9.4 %all_to_all.67.received_ref = bf16[8,16,80]{2,1,0:T(8,128)(2,1)} all-to-all(bf16[8,16,80]{2,1,0:T(8,128)(2,1)} %get-tuple-element.16), channel_id=1, replica_groups=mesh['y1'=2,'y0'=2,'z3'=2,'z2'=2,'z1'=2,'z0'=2,'x'=4,'core'=2] {'x','core'}, dimensions={0} | all-to-all | bytes 40960 | tf_op jit(solution)/shard_map/all_to_all | solution.py:103
  169.4 2.6 %shard_map.55 = bf16[16,16,80]{2,1,0:T(8,128)(2,1)} custom-call(s32[2]{0:T(128)} %pad_add_fusion.place_ref, s32[1,30]{1,0:T(1,128)} %mask.7, bf16[8,16,80]{2,1,0:T(8,128)(2,1)} %all_to_all.67.received_ref, f32[5,2,16,40]{3,2,1,0:T(8,128)} %rhs_ref.9, bf16[2,320,1200]{2,1,0:T(8,128)(2,1)} %matrix.16), custom_call_target="tpu_custom_call" | custom-call | tf_op jit(solution)/shard_map/pallas_call | solution.py:26
  171.9 17.0 %all_to_all.68.received_ref = bf16[16,16,80]{2,1,0:T(8,128)(2,1)} all-to-all(bf16[16,16,80]{2,1,0:T(8,128)(2,1)} %shard_map.55), channel_id=1, replica_groups=mesh['y1'=2,'y0'=2,'z3'=2,'z2'=2,'z1'=2,'z0'=2,'x'=4,'core'=2] {'z3','z2..., dimensions={0} | all-to-all | bytes 81920 | tf_op jit(solution)/shard_map/all_to_all | solution.py:103
  189.0 1.5 shard_map.56
  190.5 9.4 %all_to_all.69.received_ref = bf16[8,16,80]{2,1,0:T(8,128)(2,1)} all-to-all(bf16[8,16,80]{2,1,0:T(8,128)(2,1)} %shard_map.56), channel_id=1, replica_groups=mesh['y1'=2,'y0'=2,'z3'=2,'z2'=2,'z1'=2,'z0'=2,'x'=4,'core'=2] {'x','core'}, dimensions={0} | all-to-all | bytes 40960 | tf_op jit(solution)/shard_map/all_to_all | solution.py:103
  199.9 3.2 %shard_map.57 = bf16[32,16,80]{2,1,0:T(8,128)(2,1)} custom-call(bf16[8,16,80]{2,1,0:T(8,128)(2,1)} %all_to_all.69.received_ref, bf16[2,320,2480]{2,1,0:T(8,128)(2,1)} %matrix.17), custom_call_target="tpu_custom_call" | custom-call | tf_op jit(solution)/shard_map/pallas_call | solution.py:26
  203.0 20.8 %all_to_all.70.received_ref = bf16[32,16,80]{2,1,0:T(8,128)(2,1)} all-to-all(bf16[32,16,80]{2,1,0:T(8,128)(2,1)} %shard_map.57), channel_id=1, replica_groups=mesh['y1'=2,'y0'=2,'z3'=2,'z2'=2,'z1'=2,'z0'=2,'x'=4,'core'=2] {'y0','z3..., dimensions={0} | all-to-all | bytes 163840 | tf_op jit(solution)/shard_map/all_to_all | solution.py:103
  223.8 1.7 shard_map.58
Async XLA Ops:
  14.4 10.1 %all-to-all-start.1 = ((bf16[16,16,80]{2,1,0:T(8,128)(2,1)}), bf16[16,16,80]{2,1,0:T(8,128)(2,1)S(1)}, u32[]{:S(2)}, u32[]{:S(2)}) async-start(bf16[16,16,80]{2,1,0:T(8,128)(2,1)} %shard_map.47), calls=%async_computation.1 | async-start | bytes 131072 | tf_op jit(solution)/shard_map/all_to_all | solution.py:103
  24.4 0.6 copy-start

commit v2 on v1

--- a/solution.py
+++ b/solution.py
@@ -28,6 +28,7 @@
         out_shape=outs,
         in_specs=specs,
         out_specs=jax.tree.map(lambda _: whole(), outs),
+        compiler_params=pltpu.CompilerParams(vmem_limit_bytes=16 * 2**20),
     )(*inputs)
 
 

time: 228 us -> 196 us (0.86)
  Pallas kernels: 32.1 us -> 7.56 us
  blocking collectives: 183 us -> 172 us
  local copies, waits for them, and re-layouts: 0.63 us -> 4.26 us
    pallas_call x13, Pallas kernels: 32.1 us -> 7.56 us  [call(): pl.pallas_call(body, out_shape=outs, in_specs=specs, out_specs=jax.tree.m...]
    all_to_all x11, blocking collectives: 183 us -> 172 us  [over(): return lax.all_to_all(value, names, 0, 0, tiled=True)]
    unnamed x2 -> x14, local copies, waits for them, and re-layouts: 0.63 us -> 4.26 us
where the time goes in v2:
time: 196 us; the launch traced here: 195 us
  blocking collectives  172 us (88%)
  Pallas kernels  7.56 us (4%)
  waiting for transfers between devices  6.07 us (3%)
  local copies, waits for them, and re-layouts  4.26 us (2%)
  starting transfers between devices  4.03 us (2%)
    all_to_all x11, blocking collectives, over(): return lax.all_to_all(value, names, 0, 0, tiled=True)  172 us
    pallas_call x13, Pallas kernels, call(): pl.pallas_call(body, out_shape=outs, in_specs=specs, out_specs=jax.tree.m...  7.56 us
    all_to_all x1, waiting for transfers between devices, over(): return lax.all_to_all(value, names, 0, 0, tiled=True)  6.07 us
    unnamed x14, local copies, waits for them, and re-layouts  4.26 us
    all_to_all x1, starting transfers between devices, over(): return lax.all_to_all(value, names, 0, 0, tiled=True)  4.03 us
  transfers between devices with their start and end apart: 1, of which 1 were waited for; matrix products, arithmetic and copies ran while one was open for 0% of the time, Pallas kernels for 0%

profile of v2, /device:TPU:24, one launch (start us, length us, event | category | flops | bytes accessed | tf_op | source)
XLA Modules:
  0.0 194.5 jit_solution(14004344795012207299)
XLA Ops:
  0.0 0.0 copy-start.4
  0.0 0.9 copy-done.4
  0.9 0.0 copy-start.5
  0.9 0.0 copy-start.6
  0.9 0.1 shard_map.46
  1.0 9.5 %all_to_all.60.received_ref = bf16[8,16,80]{2,1,0:T(8,128)(2,1)S(1)} all-to-all(bf16[8,16,80]{2,1,0:T(8,128)(2,1)S(1)} %shard_map.46), channel_id=1, replica_groups=mesh['y1'=2,'y0'=2,'z3'=2,'z2'=2,'z1'=2,'z0'=2,'x'=4,'core'=2] {'x','core'}, dimensions={0} | all-to-all | bytes 40960 | tf_op jit(solution)/shard_map/all_to_all | solution.py:104
  10.5 0.0 copy-start
  10.5 1.9 copy-done
  12.4 0.0 copy-start.1
  12.4 1.0 shard_map.47
  13.4 4.0 %all-to-all-start.1 = ((bf16[16,16,80]{2,1,0:T(8,128)(2,1)}), bf16[16,16,80]{2,1,0:T(8,128)(2,1)S(1)}, u32[]{:S(2)}, u32[]{:S(2)}) async-start(bf16[16,16,80]{2,1,0:T(8,128)(2,1)} %shard_map.47), calls=%async_computation.1 | async-start | bytes 131072 | tf_op jit(solution)/shard_map/all_to_all | solution.py:104
  17.5 0.1 pad_add_fusion.place_ref
  17.6 6.1 %all-to-all-done.1.received_ref = bf16[16,16,80]{2,1,0:T(8,128)(2,1)S(1)} async-done(((bf16[16,16,80]{2,1,0:T(8,128)(2,1)}), bf16[16,16,80]{2,1,0:T(8,128)(2,1)S(1)}, u32[]{:S(2)}, u32[]{:S(2)}) %all-to-all-start.1) | async-done | bytes 40992 | tf_op jit(solution)/shard_map/all_to_all | solution.py:104
  23.6 0.0 copy-done.5
  23.6 0.0 copy-done.6
  23.6 0.0 copy-start.2
  23.6 1.4 copy-done.2
  25.1 0.0 copy-start.3
  25.1 0.9 shard_map.48
  26.0 8.7 %all_to_all.61.received_ref = bf16[16,16,80]{2,1,0:T(8,128)(2,1)S(1)} all-to-all(bf16[16,16,80]{2,1,0:T(8,128)(2,1)S(1)} %get-tuple-element.13), channel_id=1, replica_groups=mesh['y1'=2,'y0'=2,'z3'=2,'z2'=2,'z1'=2,'z0'=2,'x'=4,'core'=2] {'z0','x'..., dimensions={0} | all-to-all | bytes 81920 | tf_op jit(solution)/shard_map/all_to_all | solution.py:104
  34.7 0.0 copy-done.1
  34.7 0.4 shard_map.49
  35.1 14.0 %all_to_all.62.received_ref = bf16[32,16,80]{2,1,0:T(8,128)(2,1)S(1)} all-to-all(bf16[32,16,80]{2,1,0:T(8,128)(2,1)S(1)} %shard_map.49), channel_id=1, replica_groups=mesh['y1'=2,'y0'=2,'z3'=2,'z2'=2,'z1'=2,'z0'=2,'x'=4,'core'=2] {'z1','z0..., dimensions={0} | all-to-all | bytes 163840 | tf_op jit(solution)/shard_map/all_to_all | solution.py:104
  49.1 0.0 copy-done.3
  49.1 0.9 shard_map.50
  50.0 12.1 %all_to_all.63.received_ref = bf16[32,16,80]{2,1,0:T(8,128)(2,1)S(1)} all-to-all(bf16[32,16,80]{2,1,0:T(8,128)(2,1)S(1)} %get-tuple-element.14), channel_id=1, replica_groups=mesh['y1'=2,'y0'=2,'z3'=2,'z2'=2,'z1'=2,'z0'=2,'x'=4,'core'=2] {'z1','z0..., dimensions={0} | all-to-all | bytes 163840 | tf_op jit(solution)/shard_map/all_to_all | solution.py:104
  62.1 0.4 shard_map.51
  62.6 30.5 %all_to_all.64.received_ref = bf16[64,16,80]{2,1,0:T(8,128)(2,1)S(1)} all-to-all(bf16[64,16,80]{2,1,0:T(8,128)(2,1)S(1)} %shard_map.51), channel_id=1, replica_groups=mesh['y1'=2,'y0'=2,'z3'=2,'z2'=2,'z1'=2,'z0'=2,'x'=4,'core'=2] {'z2','z1..., dimensions={0} | all-to-all | bytes 327680 | tf_op jit(solution)/shard_map/all_to_all | solution.py:104
  93.1 1.0 shard_map.52
  94.1 25.6 %all_to_all.65.received_ref = bf16[64,16,80]{2,1,0:T(8,128)(2,1)S(1)} all-to-all(bf16[64,16,80]{2,1,0:T(8,128)(2,1)S(1)} %get-tuple-element.15), channel_id=1, replica_groups=mesh['y1'=2,'y0'=2,'z3'=2,'z2'=2,'z1'=2,'z0'=2,'x'=4,'core'=2] {'z2','z1..., dimensions={0} | all-to-all | bytes 327680 | tf_op jit(solution)/shard_map/all_to_all | solution.py:104
  119.7 0.4 shard_map.53
  120.1 21.0 %all_to_all.66.received_ref = bf16[16,16,80]{2,1,0:T(8,128)(2,1)S(1)} all-to-all(bf16[16,16,80]{2,1,0:T(8,128)(2,1)S(1)} %shard_map.53), channel_id=1, replica_groups=mesh['y1'=2,'y0'=2,'z3'=2,'z2'=2,'z1'=2,'z0'=2,'x'=4,'core'=2] {'z3','z2..., dimensions={0} | all-to-all | bytes 81920 | tf_op jit(solution)/shard_map/all_to_all | solution.py:104
  141.2 0.1 shard_map.54
  141.3 7.8 %all_to_all.67.received_ref = bf16[8,16,80]{2,1,0:T(8,128)(2,1)S(1)} all-to-all(bf16[8,16,80]{2,1,0:T(8,128)(2,1)S(1)} %get-tuple-element.16), channel_id=1, replica_groups=mesh['y1'=2,'y0'=2,'z3'=2,'z2'=2,'z1'=2,'z0'=2,'x'=4,'core'=2] {'x','core'}, dimensions={0} | all-to-all | bytes 40960 | tf_op jit(solution)/shard_map/all_to_all | solution.py:104
  149.1 1.0 shard_map.55
  150.1 15.4 %all_to_all.68.received_ref = bf16[16,16,80]{2,1,0:T(8,128)(2,1)S(1)} all-to-all(bf16[16,16,80]{2,1,0:T(8,128)(2,1)S(1)} %shard_map.55), channel_id=1, replica_groups=mesh['y1'=2,'y0'=2,'z3'=2,'z2'=2,'z1'=2,'z0'=2,'x'=4,'core'=2] {'z3','z2..., dimensions={0} | all-to-all | bytes 81920 | tf_op jit(solution)/shard_map/all_to_all | solution.py:104
  165.5 7.8 %all_to_all.69.received_ref = bf16[8,16,80]{2,1,0:T(8,128)(2,1)S(1)} all-to-all(bf16[8,16,80]{2,1,0:T(8,128)(2,1)S(1)} %shard_map.56), channel_id=1, replica_groups=mesh['y1'=2,'y0'=2,'z3'=2,'z2'=2,'z1'=2,'z0'=2,'x'=4,'core'=2] {'x','core'}, dimensions={0} | all-to-all | bytes 40960 | tf_op jit(solution)/shard_map/all_to_all | solution.py:104
  173.3 0.6 shard_map.57
  173.9 19.9 %all_to_all.70.received_ref = bf16[32,16,80]{2,1,0:T(8,128)(2,1)S(1)} all-to-all(bf16[32,16,80]{2,1,0:T(8,128)(2,1)S(1)} %shard_map.57), channel_id=1, replica_groups=mesh['y1'=2,'y0'=2,'z3'=2,'z2'=2,'z1'=2,'z0'=2,'x'=4,'core'=2] {'y0','z3..., dimensions={0} | all-to-all | bytes 163840 | tf_op jit(solution)/shard_map/all_to_all | solution.py:104
  193.8 0.7 shard_map.58
  (1 shorter events, 0.0 us)
Async XLA Ops:
  0.0 0.9 copy-start.4
  0.9 22.7 %copy-start.5 = (f32[5,2,16,40]{3,2,1,0:T(8,128)S(1)}, f32[5,2,16,40]{3,2,1,0:T(8,128)}, u32[]{:S(2)}) copy-start(f32[5,2,16,40]{3,2,1,0:T(8,128)} %rhs_ref.9) | copy-start | bytes 76804
  0.9 22.7 %copy-start.6 = (s32[1,30]{1,0:T(1,128)S(1)}, s32[1,30]{1,0:T(1,128)}, u32[]{:S(2)}) copy-start(s32[1,30]{1,0:T(1,128)} %mask.7) | copy-start | bytes 364
  10.5 1.9 copy-start
  12.4 22.3 %copy-start.1 = (bf16[2,320,2480]{2,1,0:T(8,128)(2,1)S(1)}, bf16[2,320,2480]{2,1,0:T(8,128)(2,1)}, u32[]{:S(2)}) copy-start(bf16[2,320,2480]{2,1,0:T(8,128)(2,1)} %matrix.17) | copy-start | bytes 9523204
  13.4 10.2 %all-to-all-start.1 = ((bf16[16,16,80]{2,1,0:T(8,128)(2,1)}), bf16[16,16,80]{2,1,0:T(8,128)(2,1)S(1)}, u32[]{:S(2)}, u32[]{:S(2)}) async-start(bf16[16,16,80]{2,1,0:T(8,128)(2,1)} %shard_map.47), calls=%async_computation.1 | async-start | bytes 131072 | tf_op jit(solution)/shard_map/all_to_all | solution.py:104
  23.6 1.4 copy-start.2
  25.1 24.0 %copy-start.3 = (bf16[2,320,1200]{2,1,0:T(8,128)(2,1)S(1)}, bf16[2,320,1200]{2,1,0:T(8,128)(2,1)}, u32[]{:S(2)}) copy-start(bf16[2,320,1200]{2,1,0:T(8,128)(2,1)} %matrix.16) | copy-start | bytes 4608004

commit v3 on v2

--- a/solution.py
+++ b/solution.py
@@ -8,7 +8,7 @@
 
 LEAF = ("y1", "y0", "z3", "z2", "z1", "z0")
 FRONT = ("x", "core")
-SPLIT = (1,)
+SPLIT = (1, 2)
 
 
 def lane_window(columns, start, width):
@@ -21,12 +21,11 @@
     return pl.BlockSpec(memory_space=space)
 
 
-def call(body, outs, inputs, scalars=0):
-    specs = [whole(pltpu.SMEM)] * scalars + [whole()] * (len(inputs) - scalars)
+def call(body, outs, inputs):
     return pl.pallas_call(
         body,
         out_shape=outs,
-        in_specs=specs,
+        in_specs=[whole()] * len(inputs),
         out_specs=jax.tree.map(lambda _: whole(), outs),
         compiler_params=pltpu.CompilerParams(vmem_limit_bytes=16 * 2**20),
     )(*inputs)
@@ -86,9 +85,6 @@
         blocks *= axes[name]
     levels, _, rhs_count, rows_dev = rhs.shape
     msg = (rhs_count, 2 * rows_dev)
-    leaf = lax.axis_index(LEAF).astype(jnp.int32)
-    front = lax.axis_index(FRONT).astype(jnp.int32)
-    place = jnp.stack([leaf, front])
     bf16 = jnp.bfloat16
 
     def sent_shape(count):
@@ -103,7 +99,7 @@
     def over(value, names):
         return lax.all_to_all(value, names, 0, 0, tiled=True)
 
-    def first_body(rhs_ref, sent):
+    def first_body(rhs_ref, inverse, upd, sent):
         put(sent, 0, message(rhs_ref[levels - 1, 0], rhs_ref[levels - 1, 1]), fronts)
 
     def invert(level, received):
@@ -123,21 +119,22 @@
         copies = 1 if level in SPLIT else fronts
         offset = blocks // 2 - 2 * members
 
-        def body(place_ref, mask, received_ref, rhs_ref, matrix, *outs):
+        def body(mask, received_ref, rhs_ref, matrix, *outs):
             sent = outs[0]
             chunks = summed_chunks(received_ref, fronts)
             if not known:
-                write_solution(outs[1], own_chunk(chunks, place_ref[1]))
+                write_solution(outs[1], own_chunk(chunks, lax.axis_index(FRONT)))
             out, shift = products(chunks, matrix, offset * rows_dev, members * rows_dev)
-            own = place_ref[0] % members
+            own = lax.axis_index(LEAF) % members
+            gates = mask[...].astype(jnp.float32)
             right = message(rhs_ref[level - 1, 0], rhs_ref[level - 1, 1])
             for a in range(members):
-                gate = mask[0, offset + a].astype(jnp.float32)
+                gate = gates[:, offset + a : offset + a + 1]
                 part = member_message(out, shift, a, rows_dev) * gate
                 put(sent, a, jnp.where(own == a, right, 0.0) - part, copies)
 
         outs = (sent_shape(members * copies),) + (() if known else (sol_shape,))
-        return call(body, outs, (place, tile_mask, received, rhs, upd_blocks), 2)
+        return call(body, outs, (tile_mask, received, rhs, upd_blocks))
 
     def combine(received, solution):
         def body(received_ref, sent, *outs):
@@ -158,7 +155,7 @@
 
         return call(body, jax.ShapeDtypeStruct(rhs.shape, jnp.float32), (received, *solved))
 
-    received = over(call(first_body, sent_shape(fronts), (rhs,)), FRONT)
+    received = over(call(first_body, sent_shape(fronts), (rhs, inv_blocks, upd_blocks)), FRONT)
     solved = [None] * levels
     for level in range(levels - 1, -1, -1):
         group = LEAF[len(LEAF) - (levels - level) :]

time: 196 us -> 185 us (0.944)
  waiting for transfers between devices: 6.07 us -> 0 us
  starting transfers between devices: 4.03 us -> 0 us
  Pallas kernels: 7.56 us -> 4.81 us
  blocking collectives: 172 us -> 174 us
    all_to_all x1 -> x0, waiting for transfers between devices: 6.07 us -> none  [over(): return lax.all_to_all(value, names, 0, 0, tiled=True)]
    all_to_all x1 -> x0, starting transfers between devices: 4.03 us -> none  [over(): return lax.all_to_all(value, names, 0, 0, tiled=True)]
    pallas_call x13 -> x15, Pallas kernels: 7.56 us -> 4.81 us  [call(): pl.pallas_call(body, out_shape=outs, in_specs=[whole()] * len(inputs), ou...]
    all_to_all x11 -> x14, blocking collectives: 172 us -> 174 us  [over(): return lax.all_to_all(value, names, 0, 0, tiled=True)]
  transfers between devices with their start and end apart: 1 -> 0, of which waited for: 1 -> 0; matrix products, arithmetic and copies ran while one was open for 0% -> 0% of each run, Pallas kernels for 0% -> 0%
where the time goes in v3:
time: 185 us; the launch traced here: 183 us
  blocking collectives  174 us (94%)
  Pallas kernels  4.81 us (3%)
  local copies, waits for them, and re-layouts  4.26 us (2%)
    all_to_all x14, blocking collectives, over(): return lax.all_to_all(value, names, 0, 0, tiled=True)  174 us
    pallas_call x15, Pallas kernels, call(): pl.pallas_call(body, out_shape=outs, in_specs=[whole()] * len(inputs), ou...  4.81 us
    unnamed x14, local copies, waits for them, and re-layouts  4.26 us

profile of v3, /device:TPU:24, one launch (start us, length us, event | category | flops | bytes accessed | tf_op | source)
XLA Modules:
  0.0 183.3 jit_solution(12438228783678289284)
XLA Ops:
  0.0 0.0 copy-start
  0.0 1.9 %copy-done = bf16[2,320,2480]{2,1,0:T(8,128)(2,1)S(1)} copy-done((bf16[2,320,2480]{2,1,0:T(8,128)(2,1)S(1)}, bf16[2,320,2480]{2,1,0:T(8,128)(2,1)}, u32[]{:S(2)}) %copy-start) | copy-done | bytes 3174424
  1.9 0.0 copy-start.2
  1.9 1.4 copy-done.2
  3.4 0.0 copy-start.4
  3.4 0.9 copy-done.4
  4.2 0.0 copy-start.1
  4.2 0.0 copy-start.3
  4.2 0.0 copy-start.6
  4.3 0.1 shard_map.46
  4.3 9.8 %all_to_all.70.received_ref = bf16[8,16,80]{2,1,0:T(8,128)(2,1)S(1)} all-to-all(bf16[8,16,80]{2,1,0:T(8,128)(2,1)S(1)} %shard_map.46), channel_id=1, replica_groups=mesh['y1'=2,'y0'=2,'z3'=2,'z2'=2,'z1'=2,'z0'=2,'x'=4,'core'=2] {'x','core'}, dimensions={0} | all-to-all | bytes 40960 | tf_op jit(solution)/shard_map/all_to_all | solution.py:100
  14.1 0.0 copy-done.1
  14.1 0.4 shard_map.47
  14.5 9.9 %all_to_all.71.received_ref = bf16[16,16,80]{2,1,0:T(8,128)(2,1)S(1)} all-to-all(bf16[16,16,80]{2,1,0:T(8,128)(2,1)S(1)} %shard_map.47), channel_id=1, replica_groups=mesh['y1'=2,'y0'=2,'z3'=2,'z2'=2,'z1'=2,'z0'=2,'x'=4,'core'=2] {'z0','x'..., dimensions={0} | all-to-all | bytes 81920 | tf_op jit(solution)/shard_map/all_to_all | solution.py:100
  24.4 0.0 copy-done.3
  24.4 0.0 copy-done.6
  24.4 0.4 shard_map.48
  24.7 8.7 %all_to_all.72.received_ref = bf16[16,16,80]{2,1,0:T(8,128)(2,1)S(1)} all-to-all(bf16[16,16,80]{2,1,0:T(8,128)(2,1)S(1)} %get-tuple-element.13), channel_id=1, replica_groups=mesh['y1'=2,'y0'=2,'z3'=2,'z2'=2,'z1'=2,'z0'=2,'x'=4,'core'=2] {'z0','x'..., dimensions={0} | all-to-all | bytes 81920 | tf_op jit(solution)/shard_map/all_to_all | solution.py:100
  33.5 0.4 shard_map.49
  33.9 0.0 copy-start.5
  33.9 14.1 %all_to_all.73.received_ref = bf16[32,16,80]{2,1,0:T(8,128)(2,1)S(1)} all-to-all(bf16[32,16,80]{2,1,0:T(8,128)(2,1)S(1)} %shard_map.49), channel_id=1, replica_groups=mesh['y1'=2,'y0'=2,'z3'=2,'z2'=2,'z1'=2,'z0'=2,'x'=4,'core'=2] {'z1','z0..., dimensions={0} | all-to-all | bytes 163840 | tf_op jit(solution)/shard_map/all_to_all | solution.py:100
  48.0 0.4 shard_map.50
  48.4 12.1 %all_to_all.74.received_ref = bf16[32,16,80]{2,1,0:T(8,128)(2,1)S(1)} all-to-all(bf16[32,16,80]{2,1,0:T(8,128)(2,1)S(1)} %get-tuple-element.14), channel_id=1, replica_groups=mesh['y1'=2,'y0'=2,'z3'=2,'z2'=2,'z1'=2,'z0'=2,'x'=4,'core'=2] {'z1','z0..., dimensions={0} | all-to-all | bytes 163840 | tf_op jit(solution)/shard_map/all_to_all | solution.py:100
  60.5 0.4 shard_map.51
  60.9 19.7 %all_to_all.75.received_ref = bf16[8,16,80]{2,1,0:T(8,128)(2,1)S(1)} all-to-all(bf16[8,16,80]{2,1,0:T(8,128)(2,1)S(1)} %shard_map.51), channel_id=1, replica_groups=mesh['y1'=2,'y0'=2,'z3'=2,'z2'=2,'z1'=2,'z0'=2,'x'=4,'core'=2] {'z2','z1..., dimensions={0} | all-to-all | bytes 40960 | tf_op jit(solution)/shard_map/all_to_all | solution.py:100
  80.6 0.1 shard_map.52
  80.7 7.8 %all_to_all.76.received_ref = bf16[8,16,80]{2,1,0:T(8,128)(2,1)S(1)} all-to-all(bf16[8,16,80]{2,1,0:T(8,128)(2,1)S(1)} %get-tuple-element.15), channel_id=1, replica_groups=mesh['y1'=2,'y0'=2,'z3'=2,'z2'=2,'z1'=2,'z0'=2,'x'=4,'core'=2] {'x','core'}, dimensions={0} | all-to-all | bytes 40960 | tf_op jit(solution)/shard_map/all_to_all | solution.py:100
  88.5 0.0 copy-done.5
  88.5 0.4 shard_map.53
  88.9 13.0 %all_to_all.77.received_ref = bf16[8,16,80]{2,1,0:T(8,128)(2,1)S(1)} all-to-all(bf16[8,16,80]{2,1,0:T(8,128)(2,1)S(1)} %shard_map.53), channel_id=1, replica_groups=mesh['y1'=2,'y0'=2,'z3'=2,'z2'=2,'z1'=2,'z0'=2,'x'=4,'core'=2] {'z2','z1..., dimensions={0} | all-to-all | bytes 40960 | tf_op jit(solution)/shard_map/all_to_all | solution.py:100
  101.9 7.8 %all_to_all.78.received_ref = bf16[8,16,80]{2,1,0:T(8,128)(2,1)S(1)} all-to-all(bf16[8,16,80]{2,1,0:T(8,128)(2,1)S(1)} %shard_map.54), channel_id=1, replica_groups=mesh['y1'=2,'y0'=2,'z3'=2,'z2'=2,'z1'=2,'z0'=2,'x'=4,'core'=2] {'x','core'}, dimensions={0} | all-to-all | bytes 40960 | tf_op jit(solution)/shard_map/all_to_all | solution.py:100
  109.8 0.4 shard_map.55
  110.2 20.2 %all_to_all.79.received_ref = bf16[16,16,80]{2,1,0:T(8,128)(2,1)S(1)} all-to-all(bf16[16,16,80]{2,1,0:T(8,128)(2,1)S(1)} %shard_map.55), channel_id=1, replica_groups=mesh['y1'=2,'y0'=2,'z3'=2,'z2'=2,'z1'=2,'z0'=2,'x'=4,'core'=2] {'z3','z2..., dimensions={0} | all-to-all | bytes 81920 | tf_op jit(solution)/shard_map/all_to_all | solution.py:100
  130.4 0.1 shard_map.56
  130.5 7.8 %all_to_all.80.received_ref = bf16[8,16,80]{2,1,0:T(8,128)(2,1)S(1)} all-to-all(bf16[8,16,80]{2,1,0:T(8,128)(2,1)S(1)} %get-tuple-element.16), channel_id=1, replica_groups=mesh['y1'=2,'y0'=2,'z3'=2,'z2'=2,'z1'=2,'z0'=2,'x'=4,'core'=2] {'x','core'}, dimensions={0} | all-to-all | bytes 40960 | tf_op jit(solution)/shard_map/all_to_all | solution.py:100
  138.3 0.5 shard_map.57
  138.8 15.5 %all_to_all.81.received_ref = bf16[16,16,80]{2,1,0:T(8,128)(2,1)S(1)} all-to-all(bf16[16,16,80]{2,1,0:T(8,128)(2,1)S(1)} %shard_map.57), channel_id=1, replica_groups=mesh['y1'=2,'y0'=2,'z3'=2,'z2'=2,'z1'=2,'z0'=2,'x'=4,'core'=2] {'z3','z2..., dimensions={0} | all-to-all | bytes 81920 | tf_op jit(solution)/shard_map/all_to_all | solution.py:100
  154.3 7.8 %all_to_all.82.received_ref = bf16[8,16,80]{2,1,0:T(8,128)(2,1)S(1)} all-to-all(bf16[8,16,80]{2,1,0:T(8,128)(2,1)S(1)} %shard_map.58), channel_id=1, replica_groups=mesh['y1'=2,'y0'=2,'z3'=2,'z2'=2,'z1'=2,'z0'=2,'x'=4,'core'=2] {'x','core'}, dimensions={0} | all-to-all | bytes 40960 | tf_op jit(solution)/shard_map/all_to_all | solution.py:100
  162.1 0.6 shard_map.59
  162.7 19.8 %all_to_all.83.received_ref = bf16[32,16,80]{2,1,0:T(8,128)(2,1)S(1)} all-to-all(bf16[32,16,80]{2,1,0:T(8,128)(2,1)S(1)} %shard_map.59), channel_id=1, replica_groups=mesh['y1'=2,'y0'=2,'z3'=2,'z2'=2,'z1'=2,'z0'=2,'x'=4,'core'=2] {'y0','z3..., dimensions={0} | all-to-all | bytes 163840 | tf_op jit(solution)/shard_map/all_to_all | solution.py:100
  182.5 0.7 shard_map.60
  (2 shorter events, 0.0 us)
Async XLA Ops:
  0.0 1.9 %copy-start = (bf16[2,320,2480]{2,1,0:T(8,128)(2,1)S(1)}, bf16[2,320,2480]{2,1,0:T(8,128)(2,1)}, u32[]{:S(2)}) copy-start(bf16[2,320,2480]{2,1,0:T(8,128)(2,1)} %matrix.17) | copy-start | bytes 9523204
  1.9 1.4 copy-start.2
  3.4 0.9 copy-start.4
  4.2 9.9 %copy-start.1 = (bf16[2,320,2480]{2,1,0:T(8,128)(2,1)S(1)}, bf16[2,320,2480]{2,1,0:T(8,128)(2,1)}, u32[]{:S(2)}) copy-start(bf16[2,320,2480]{2,1,0:T(8,128)(2,1)} %matrix.17) | copy-start | bytes 9523204
  4.2 20.1 %copy-start.3 = (bf16[2,320,1200]{2,1,0:T(8,128)(2,1)S(1)}, bf16[2,320,1200]{2,1,0:T(8,128)(2,1)}, u32[]{:S(2)}) copy-start(bf16[2,320,1200]{2,1,0:T(8,128)(2,1)} %matrix.16) | copy-start | bytes 4608004
  4.2 20.1 %copy-start.6 = (s32[1,30]{1,0:T(1,128)S(1)}, s32[1,30]{1,0:T(1,128)}, u32[]{:S(2)}) copy-start(s32[1,30]{1,0:T(1,128)} %mask.7) | copy-start | bytes 364
  33.9 54.6 %copy-start.5 = (f32[5,2,16,40]{3,2,1,0:T(8,128)S(1)}, f32[5,2,16,40]{3,2,1,0:T(8,128)}, u32[]{:S(2)}) copy-start(f32[5,2,16,40]{3,2,1,0:T(8,128)} %rhs_ref.9) | copy-start | bytes 76804

commit v4 on v3

--- a/solution.py
+++ b/solution.py
@@ -99,20 +99,24 @@
     def over(value, names):
         return lax.all_to_all(value, names, 0, 0, tiled=True)
 
-    def first_body(rhs_ref, inverse, upd, sent):
+    def first_body(rhs_ref, sent):
         put(sent, 0, message(rhs_ref[levels - 1, 0], rhs_ref[levels - 1, 1]), fronts)
 
-    def invert(level, received):
+    def fetch_body(inverse, upd, mask, rhs_ref, token):
+        token[...] = jnp.zeros(token.shape, token.dtype)
+
+    def invert(level, received, tokens=()):
         members = blocks >> (level + 1)
         copies = 1 if level in SPLIT or level == 0 else fronts
 
-        def body(received_ref, matrix, sent):
+        def body(received_ref, matrix, *refs):
+            sent = refs[-1]
             chunks = summed_chunks(received_ref, fronts)
             out, shift = products(chunks, matrix, (blocks - 2 * members) * rows_dev, members * rows_dev)
             for a in range(members):
                 put(sent, a, member_message(out, shift, a, rows_dev), copies)
 
-        return call(body, sent_shape(members * copies), (received, inv_blocks))
+        return call(body, sent_shape(members * copies), (received, inv_blocks, *tokens))
 
     def update(level, received, known):
         members = blocks >> (level + 1)
@@ -155,11 +159,12 @@
 
         return call(body, jax.ShapeDtypeStruct(rhs.shape, jnp.float32), (received, *solved))
 
-    received = over(call(first_body, sent_shape(fronts), (rhs, inv_blocks, upd_blocks)), FRONT)
+    token = call(fetch_body, jax.ShapeDtypeStruct((8, 128), jnp.float32), (inv_blocks, upd_blocks, tile_mask, rhs))
+    received = over(call(first_body, sent_shape(fronts), (rhs,)), FRONT)
     solved = [None] * levels
     for level in range(levels - 1, -1, -1):
         group = LEAF[len(LEAF) - (levels - level) :]
-        sent = invert(level, received)
+        sent = invert(level, received, (token,) if level == levels - 1 else ())
         if level == 0:
             return finish(over(sent, group), solved[1:])
         if level in SPLIT:

time: 185 us -> 186 us (level)
  blocking collectives: 174 us -> 167 us
  starting transfers between devices: 0 us -> 4.3 us
  local copies, waits for them, and re-layouts: 4.26 us -> 7.17 us
    all_to_all x14 -> x13, blocking collectives: 174 us -> 167 us  [over(): return lax.all_to_all(value, names, 0, 0, tiled=True)]
    all_to_all x0 -> x1, starting transfers between devices: none -> 4.3 us  [over(): return lax.all_to_all(value, names, 0, 0, tiled=True)]
    unnamed x14 -> x18, local copies, waits for them, and re-layouts: 4.26 us -> 7.17 us
    pallas_call x15 -> x16, Pallas kernels: 4.81 us -> 5.42 us  [call(): pl.pallas_call(body, out_shape=outs, in_specs=[whole()] * len(inputs), ou...]
  transfers between devices with their start and end apart: 0 -> 1, of which waited for: 0 -> 1; matrix products, arithmetic and copies ran while one was open for 0% -> 0% of each run, Pallas kernels for 0% -> 0%
where the time goes in v4:
time: 186 us; the launch traced here: 184 us
  blocking collectives  167 us (90%)
  local copies, waits for them, and re-layouts  7.17 us (4%)
  Pallas kernels  5.42 us (3%)
  starting transfers between devices  4.3 us (2%)
    all_to_all x13, blocking collectives, over(): return lax.all_to_all(value, names, 0, 0, tiled=True)  167 us
    unnamed x18, local copies, waits for them, and re-layouts  7.17 us
    pallas_call x16, Pallas kernels, call(): pl.pallas_call(body, out_shape=outs, in_specs=[whole()] * len(inputs), ou...  5.42 us
    all_to_all x1, starting transfers between devices, over(): return lax.all_to_all(value, names, 0, 0, tiled=True)  4.3 us
  transfers between devices with their start and end apart: 1, of which 1 were waited for; matrix products, arithmetic and copies ran while one was open for 0% of the time, Pallas kernels for 0%

profile of v4, /device:TPU:24, one launch (start us, length us, event | category | flops | bytes accessed | tf_op | source)
XLA Modules:
  0.0 184.2 jit_solution(4827085615998856318)
XLA Ops:
  0.0 0.0 copy-start.4
  0.0 0.9 copy-done.4
  0.9 0.7 shard_map.46
  1.6 4.3 %all-to-all-start = ((bf16[8,16,80]{2,1,0:T(8,128)(2,1)}), bf16[8,16,80]{2,1,0:T(8,128)(2,1)S(1)}, u32[]{:S(2)}, u32[]{:S(2)}) async-start(bf16[8,16,80]{2,1,0:T(8,128)(2,1)} %shard_map.46), calls=%async_computation | async-start | bytes 65536 | tf_op jit(solution)/shard_map/all_to_all | solution.py:100
  5.9 0.0 copy-start
  5.9 1.9 %copy-done = bf16[2,320,2480]{2,1,0:T(8,128)(2,1)S(1)} copy-done((bf16[2,320,2480]{2,1,0:T(8,128)(2,1)S(1)}, bf16[2,320,2480]{2,1,0:T(8,128)(2,1)}, u32[]{:S(2)}) %copy-start) | copy-done | bytes 3174424
  7.8 0.0 copy-start.2
  7.8 1.4 copy-done.2
  9.2 0.0 copy-start.5
  9.2 0.9 copy-done.5
  10.1 0.0 copy-start.7
  10.1 0.7 copy-done.7
  10.8 0.0 copy-start.1
  10.8 0.0 copy-start.6
  10.8 0.0 copy-start.8
  10.8 0.5 all-to-all-done.received_ref
  11.3 1.4 copy-done.1
  12.7 0.0 copy-start.3
  12.7 0.4 shard_map.48
  13.1 12.4 %all_to_all.70.received_ref = bf16[16,16,80]{2,1,0:T(8,128)(2,1)S(1)} all-to-all(bf16[16,16,80]{2,1,0:T(8,128)(2,1)S(1)} %shard_map.48), channel_id=1, replica_groups=mesh['y1'=2,'y0'=2,'z3'=2,'z2'=2,'z1'=2,'z0'=2,'x'=4,'core'=2] {'z0','x'..., dimensions={0} | all-to-all | bytes 81920 | tf_op jit(solution)/shard_map/all_to_all | solution.py:100
  25.4 0.0 copy-done.6
  25.4 0.0 copy-done.8
  25.4 0.0 copy-done.3
  25.4 0.4 shard_map.49
  25.8 8.7 %all_to_all.71.received_ref = bf16[16,16,80]{2,1,0:T(8,128)(2,1)S(1)} all-to-all(bf16[16,16,80]{2,1,0:T(8,128)(2,1)S(1)} %get-tuple-element.13), channel_id=1, replica_groups=mesh['y1'=2,'y0'=2,'z3'=2,'z2'=2,'z1'=2,'z0'=2,'x'=4,'core'=2] {'z0','x'..., dimensions={0} | all-to-all | bytes 81920 | tf_op jit(solution)/shard_map/all_to_all | solution.py:100
  34.5 0.4 shard_map.50
  34.9 14.0 %all_to_all.72.received_ref = bf16[32,16,80]{2,1,0:T(8,128)(2,1)S(1)} all-to-all(bf16[32,16,80]{2,1,0:T(8,128)(2,1)S(1)} %shard_map.50), channel_id=1, replica_groups=mesh['y1'=2,'y0'=2,'z3'=2,'z2'=2,'z1'=2,'z0'=2,'x'=4,'core'=2] {'z1','z0..., dimensions={0} | all-to-all | bytes 163840 | tf_op jit(solution)/shard_map/all_to_all | solution.py:100
  48.9 0.4 shard_map.51
  49.3 12.1 %all_to_all.73.received_ref = bf16[32,16,80]{2,1,0:T(8,128)(2,1)S(1)} all-to-all(bf16[32,16,80]{2,1,0:T(8,128)(2,1)S(1)} %get-tuple-element.14), channel_id=1, replica_groups=mesh['y1'=2,'y0'=2,'z3'=2,'z2'=2,'z1'=2,'z0'=2,'x'=4,'core'=2] {'z1','z0..., dimensions={0} | all-to-all | bytes 163840 | tf_op jit(solution)/shard_map/all_to_all | solution.py:100
  61.4 0.4 shard_map.52
  61.9 19.7 %all_to_all.74.received_ref = bf16[8,16,80]{2,1,0:T(8,128)(2,1)S(1)} all-to-all(bf16[8,16,80]{2,1,0:T(8,128)(2,1)S(1)} %shard_map.52), channel_id=1, replica_groups=mesh['y1'=2,'y0'=2,'z3'=2,'z2'=2,'z1'=2,'z0'=2,'x'=4,'core'=2] {'z2','z1..., dimensions={0} | all-to-all | bytes 40960 | tf_op jit(solution)/shard_map/all_to_all | solution.py:100
  81.5 0.1 shard_map.53
  81.6 7.8 %all_to_all.75.received_ref = bf16[8,16,80]{2,1,0:T(8,128)(2,1)S(1)} all-to-all(bf16[8,16,80]{2,1,0:T(8,128)(2,1)S(1)} %get-tuple-element.15), channel_id=1, replica_groups=mesh['y1'=2,'y0'=2,'z3'=2,'z2'=2,'z1'=2,'z0'=2,'x'=4,'core'=2] {'x','core'}, dimensions={0} | all-to-all | bytes 40960 | tf_op jit(solution)/shard_map/all_to_all | solution.py:100
  89.4 0.4 shard_map.54
  89.8 13.0 %all_to_all.76.received_ref = bf16[8,16,80]{2,1,0:T(8,128)(2,1)S(1)} all-to-all(bf16[8,16,80]{2,1,0:T(8,128)(2,1)S(1)} %shard_map.54), channel_id=1, replica_groups=mesh['y1'=2,'y0'=2,'z3'=2,'z2'=2,'z1'=2,'z0'=2,'x'=4,'core'=2] {'z2','z1..., dimensions={0} | all-to-all | bytes 40960 | tf_op jit(solution)/shard_map/all_to_all | solution.py:100
  102.9 7.8 %all_to_all.77.received_ref = bf16[8,16,80]{2,1,0:T(8,128)(2,1)S(1)} all-to-all(bf16[8,16,80]{2,1,0:T(8,128)(2,1)S(1)} %shard_map.55), channel_id=1, replica_groups=mesh['y1'=2,'y0'=2,'z3'=2,'z2'=2,'z1'=2,'z0'=2,'x'=4,'core'=2] {'x','core'}, dimensions={0} | all-to-all | bytes 40960 | tf_op jit(solution)/shard_map/all_to_all | solution.py:100
  110.7 0.4 shard_map.56
  111.1 20.2 %all_to_all.78.received_ref = bf16[16,16,80]{2,1,0:T(8,128)(2,1)S(1)} all-to-all(bf16[16,16,80]{2,1,0:T(8,128)(2,1)S(1)} %shard_map.56), channel_id=1, replica_groups=mesh['y1'=2,'y0'=2,'z3'=2,'z2'=2,'z1'=2,'z0'=2,'x'=4,'core'=2] {'z3','z2..., dimensions={0} | all-to-all | bytes 81920 | tf_op jit(solution)/shard_map/all_to_all | solution.py:100
  131.3 0.1 shard_map.57
  131.4 7.8 %all_to_all.79.received_ref = bf16[8,16,80]{2,1,0:T(8,128)(2,1)S(1)} all-to-all(bf16[8,16,80]{2,1,0:T(8,128)(2,1)S(1)} %get-tuple-element.16), channel_id=1, replica_groups=mesh['y1'=2,'y0'=2,'z3'=2,'z2'=2,'z1'=2,'z0'=2,'x'=4,'core'=2] {'x','core'}, dimensions={0} | all-to-all | bytes 40960 | tf_op jit(solution)/shard_map/all_to_all | solution.py:100
  139.2 0.5 shard_map.58
  139.7 15.5 %all_to_all.80.received_ref = bf16[16,16,80]{2,1,0:T(8,128)(2,1)S(1)} all-to-all(bf16[16,16,80]{2,1,0:T(8,128)(2,1)S(1)} %shard_map.58), channel_id=1, replica_groups=mesh['y1'=2,'y0'=2,'z3'=2,'z2'=2,'z1'=2,'z0'=2,'x'=4,'core'=2] {'z3','z2..., dimensions={0} | all-to-all | bytes 81920 | tf_op jit(solution)/shard_map/all_to_all | solution.py:100
  155.2 7.8 %all_to_all.81.received_ref = bf16[8,16,80]{2,1,0:T(8,128)(2,1)S(1)} all-to-all(bf16[8,16,80]{2,1,0:T(8,128)(2,1)S(1)} %shard_map.59), channel_id=1, replica_groups=mesh['y1'=2,'y0'=2,'z3'=2,'z2'=2,'z1'=2,'z0'=2,'x'=4,'core'=2] {'x','core'}, dimensions={0} | all-to-all | bytes 40960 | tf_op jit(solution)/shard_map/all_to_all | solution.py:100
  163.1 0.6 shard_map.60
  163.6 19.8 %all_to_all.82.received_ref = bf16[32,16,80]{2,1,0:T(8,128)(2,1)S(1)} all-to-all(bf16[32,16,80]{2,1,0:T(8,128)(2,1)S(1)} %shard_map.60), channel_id=1, replica_groups=mesh['y1'=2,'y0'=2,'z3'=2,'z2'=2,'z1'=2,'z0'=2,'x'=4,'core'=2] {'y0','z3..., dimensions={0} | all-to-all | bytes 163840 | tf_op jit(solution)/shard_map/all_to_all | solution.py:100
  183.5 0.7 shard_map.61
  (3 shorter events, 0.0 us)
Async XLA Ops:
  0.0 0.9 copy-start.4
  1.6 9.7 %all-to-all-start = ((bf16[8,16,80]{2,1,0:T(8,128)(2,1)}), bf16[8,16,80]{2,1,0:T(8,128)(2,1)S(1)}, u32[]{:S(2)}, u32[]{:S(2)}) async-start(bf16[8,16,80]{2,1,0:T(8,128)(2,1)} %shard_map.46), calls=%async_computation | async-start | bytes 65536 | tf_op jit(solution)/shard_map/all_to_all | solution.py:100
  5.9 1.9 %copy-start = (bf16[2,320,2480]{2,1,0:T(8,128)(2,1)S(1)}, bf16[2,320,2480]{2,1,0:T(8,128)(2,1)}, u32[]{:S(2)}) copy-start(bf16[2,320,2480]{2,1,0:T(8,128)(2,1)} %matrix.17) | copy-start | bytes 9523204
  7.8 1.4 copy-start.2
  9.2 0.9 copy-start.5
  10.1 0.7 copy-start.7
  10.8 1.9 %copy-start.1 = (bf16[2,320,2480]{2,1,0:T(8,128)(2,1)S(1)}, bf16[2,320,2480]{2,1,0:T(8,128)(2,1)}, u32[]{:S(2)}) copy-start(bf16[2,320,2480]{2,1,0:T(8,128)(2,1)} %matrix.17) | copy-start | bytes 9523204
  10.8 14.7 %copy-start.6 = (f32[5,2,16,40]{3,2,1,0:T(8,128)S(1)}, f32[5,2,16,40]{3,2,1,0:T(8,128)}, u32[]{:S(2)}) copy-start(f32[5,2,16,40]{3,2,1,0:T(8,128)} %rhs_ref.11) | copy-start | bytes 76804
  10.8 14.7 %copy-start.8 = (s32[1,30]{1,0:T(1,128)S(1)}, s32[1,30]{1,0:T(1,128)}, u32[]{:S(2)}) copy-start(s32[1,30]{1,0:T(1,128)} %mask.9) | copy-start | bytes 364
  12.7 12.7 %copy-start.3 = (bf16[2,320,1200]{2,1,0:T(8,128)(2,1)S(1)}, bf16[2,320,1200]{2,1,0:T(8,128)(2,1)}, u32[]{:S(2)}) copy-start(bf16[2,320,1200]{2,1,0:T(8,128)(2,1)} %matrix.16) | copy-start | bytes 4608004

commit v5 on v3

v5 whole, which is shorter than its diff:
```python
import jax
import jax.numpy as jnp
from jax import lax
from jax.experimental import pallas as pl
from jax.experimental.pallas import tpu as pltpu
from jax.sharding import Mesh
from jax.sharding import PartitionSpec as P

LEAF = ("y1", "y0", "z3", "z2", "z1", "z0")
FRONT = ("x", "core")
WITH_FRONT, THEN_FRONT, WITH_X_THEN_CORE = range(3)
WAY = {4: WITH_FRONT, 3: WITH_FRONT, 2: WITH_X_THEN_CORE, 1: THEN_FRONT}
STRIP = 4


def lane_window(columns, start, width):
    first = start // 128 * 128
    last = min(-(-(start + width) // 128) * 128, columns)
    return first, last


def whole(space=pltpu.VMEM):
    return pl.BlockSpec(memory_space=space)


def call(body, outs, inputs, space=pltpu.VMEM, scratch=()):
    return pl.pallas_call(
        body,
        out_shape=outs,
        in_specs=[whole(space)] * len(inputs),
        out_specs=jax.tree.map(lambda _: whole(), outs),
        scratch_shapes=scratch,
        compiler_params=pltpu.CompilerParams(vmem_limit_bytes=16 * 2**20),
    )(*inputs)


class Packing:
    def __init__(self, rows, lanes):
        self.rows, self.lanes = rows, lanes
        self.groups = 128 // lanes
        self.strips = -(-rows // (self.groups * STRIP))
        self.shape = (self.strips, STRIP, self.groups * lanes)

    def first_row(self, group, strip):
        return (group * self.strips + strip) * STRIP

    def pack(self, block):
        strips = []
        for j in range(self.strips):
            pieces = []
            for g in range(self.groups):
                row = self.first_row(g, j)
                if row < self.rows:
                    pieces.append(block[row : row + STRIP])
                else:
                    pieces.append(jnp.zeros((STRIP, self.lanes), jnp.float32))
            strips.append(jnp.concatenate(pieces, axis=1))
        return strips

    def unpack(self, chunks):
        rows = []
        for g in range(self.groups):
            for j in range(self.strips):
                if self.first_row(g, j) < self.rows:
                    low = g * self.lanes
                    rows.append(jnp.concatenate([c[j][:, low : low + self.lanes] for c in chunks], axis=1))
        return jnp.concatenate(rows, axis=0)


def summed_chunks(received, order):
    chunks = []
    for messages in order:
        strips = []
        for j in range(received.shape[1]):
            total = received[messages[0], j].astype(jnp.float32)
            for m in messages[1:]:
                total = total + received[m, j].astype(jnp.float32)
            strips.append(total)
        chunks.append(strips)
    return chunks


def own_chunk(chunks, own):
    strips = []
    for j in range(len(chunks[0])):
        total = jnp.zeros(chunks[0][j].shape, jnp.float32)
        for c in range(len(chunks)):
            total = total + jnp.where(own == c, chunks[c][j], 0.0)
        strips.append(total)
    return strips


def products(block, matrix, start, width):
    half = block.shape[0] // 2
    real, imag = block[:half], block[half:]
    upper = jnp.concatenate([real, -imag], axis=1)
    lower = jnp.concatenate([imag, real], axis=1)
    stacked = jnp.concatenate([upper, lower], axis=0).astype(jnp.bfloat16)
    first, last = lane_window(matrix.shape[2], start, width)
    weights = matrix[:, :, first:last].reshape(-1, last - first)
    return jnp.dot(stacked, weights, preferred_element_type=jnp.float32), start - first


def put(sent, slots, strips):
    for j, strip in enumerate(strips):
        value = strip.astype(jnp.bfloat16)
        for slot in slots:
            sent[slot, j] = value


def shards(rhs, inv_blocks, upd_blocks, tile_mask):
    axes = {name: lax.axis_size(name) for name in LEAF + FRONT}
    fronts = axes["x"] * axes["core"]
    blocks = 1
    for name in LEAF:
        blocks *= axes[name]
    levels, _, rhs_count, rows_dev = rhs.shape
    packing = Packing(2 * rhs_count, rows_dev)

    def sent_shape(count):
        return jax.ShapeDtypeStruct((count,) + packing.shape, jnp.bfloat16)

    sol_shape = jax.ShapeDtypeStruct((2, rhs_count, rows_dev), jnp.float32)

    def both_parts(rhs_ref, level):
        return jnp.concatenate([rhs_ref[level, 0], rhs_ref[level, 1]], axis=0)

    def write_solution(sol, strips):
        value = packing.unpack([strips])
        sol[0] = value[:rhs_count]
        sol[1] = value[rhs_count:]

    def over(value, names):
        return lax.all_to_all(value, names, 0, 0, tiled=True)

    def by_front(count):
        return [[m * fronts + c for m in range(count)] for c in range(fronts)]

    def copies_of(way):
        return {WITH_FRONT: fronts, WITH_X_THEN_CORE: axes["x"], THEN_FRONT: 1}[way]

    def first_body(rhs_hbm, inv_hbm, upd_hbm, mask_hbm, sent, rhs_ref, inverse, upd, mask, sems):
        pairs = ((rhs_hbm, rhs_ref), (inv_hbm, inverse), (upd_hbm, upd), (mask_hbm, mask))
        moves = [pltpu.make_async_copy(a, b, sems.at[k]) for k, (a, b) in enumerate(pairs)]
        for move in moves:
            move.start()
        moves[0].wait()
        put(sent, range(fronts), packing.pack(both_parts(rhs_ref, levels - 1)))
        for move in moves[1:]:
            move.wait()

    def same(array):
        return jax.ShapeDtypeStruct(array.shape, array.dtype)

    sent, rhs, inv_blocks, upd_blocks, tile_mask = call(
        first_body,
        (sent_shape(fronts), same(rhs), same(inv_blocks), same(upd_blocks), same(tile_mask)),
        [pltpu.with_memory_space_constraint(a, pltpu.HBM) for a in (rhs, inv_blocks, upd_blocks, tile_mask)],
        pltpu.HBM,
        (pltpu.SemaphoreType.DMA((4,)),),
    )

    def invert(level, received, order):
        members = blocks >> (level + 1)
        copies = copies_of(WAY[level]) if level > 0 else 1

        def body(received_ref, matrix, sent):
            block = packing.unpack(summed_chunks(received_ref, order))
            out, shift = products(block, matrix, (blocks - 2 * members) * rows_dev, members * rows_dev)
            for a in range(members):
                lane = shift + a * rows_dev
                strips = packing.pack(out[:, lane : lane + rows_dev])
                put(sent, range(a * copies, (a + 1) * copies), strips)

        return call(body, sent_shape(members * copies), (received, inv_blocks))

    def update(level, received, order, known):
        members = blocks >> (level + 1)
        copies = copies_of(WAY[level])
        offset = blocks // 2 - 2 * members

        def body(mask, received_ref, rhs_ref, matrix, *outs):
            sent = outs[0]
            chunks = summed_chunks(received_ref, order)
            if not known:
                write_solution(outs[1], own_chunk(chunks, lax.axis_index(FRONT)))
            out, shift = products(packing.unpack(chunks), matrix, offset * rows_dev, members * rows_dev)
            own = lax.axis_index(LEAF) % members
            gates = mask[...].astype(jnp.float32)
            right = both_parts(rhs_ref, level - 1)
            for a in range(members):
                lane = shift + a * rows_dev
                part = out[:, lane : lane + rows_dev] * gates[:, offset + a : offset + a + 1]
                strips = packing.pack(jnp.where(own == a, right, 0.0) - part)
                put(sent, range(a * copies, (a + 1) * copies), strips)

        outs = (sent_shape(members * copies),) + (() if known else (sol_shape,))
        return call(body, outs, (tile_mask, received, rhs, upd_blocks))

    def combine(level, received, solution):
        members = blocks >> (level + 1)
        kept = copies_of(WAY[level])
        copies = fronts if WAY[level] == THEN_FRONT else 1

        def body(received_ref, sent, *outs):
            chunks = summed_chunks(received_ref, [[m * kept + k for m in range(members)] for k in range(kept)])
            if solution:
                own = lax.axis_index("x") if kept > 1 else 0
                write_solution(outs[0], own_chunk(chunks, own))
            for k in range(kept):
                put(sent, range(k * copies, (k + 1) * copies), chunks[k])

        outs = (sent_shape(kept * copies),) + ((sol_shape,) if solution else ())
        return call(body, outs, (received,))

    def exchange(level, sent, solution):
        members = blocks >> (level + 1)
        group = LEAF[len(LEAF) - (levels - level) :]
        if WAY[level] == WITH_FRONT:
            return over(sent, group + FRONT), by_front(members), None
        if WAY[level] == THEN_FRONT:
            sent, *solved = combine(level, over(sent, group), solution)
            return over(sent, FRONT), by_front(1), solved[0] if solution else None
        sent, *solved = combine(level, over(sent, group + FRONT[:1]), solution)
        both = lax.all_gather(sent, FRONT[1], axis=0, tiled=True)
        order = [[(c % axes["core"]) * axes["x"] + c // axes["core"]] for c in range(fronts)]
        return both, order, solved[0] if solution else None

    def finish(received, solved):
        def body(received_ref, *refs):
            out = refs[-1]
            write_solution(out.at[0], summed_chunks(received_ref, [range(received.shape[0])])[0])
            for level in range(1, levels):
                out[level] = refs[level - 1][...]

        return call(body, same(rhs), (received, *solved))

    received, order = over(sent, FRONT), by_front(1)
    solved = [None] * levels
    for level in range(levels - 1, 0, -1):
        received, order, solved[level] = exchange(level, invert(level, received, order), True)
        sent, *rest = update(level, received, order, solved[level] is not None)
        if rest:
            solved[level] = rest[0]
        received, order, _ = exchange(level, sent, False)
    return finish(over(invert(0, received, order), LEAF[1:]), solved[1:])


def solution(mesh):
    finer = Mesh(mesh.devices.reshape(2, 2, 2, 2, 2, 2, 4, 2), LEAF + FRONT)
    placed = (
        P(None, None, None, LEAF + FRONT),
        P(None, LEAF, FRONT),
        P(None, LEAF, FRONT),
        P(LEAF, None),
    )
    return jax.shard_map(
        shards,
        mesh=finer,
        in_specs=placed,
        out_specs=P(None, None, None, LEAF + FRONT),
        check_vma=False,
    )
```

time: 185 us -> 176 us (0.951)
  blocking collectives: 174 us -> 168 us
  local copies, waits for them, and re-layouts: 4.26 us -> 0 us
  Pallas kernels: 4.81 us -> 7.68 us
    all_to_all x14 -> x12, blocking collectives: 174 us -> 164 us  [over(): return lax.all_to_all(value, names, 0, 0, tiled=True)]
    unnamed x14 -> x0, local copies, waits for them, and re-layouts: 4.26 us -> none
    all_gather x0 -> x2, blocking collectives: none -> 3.65 us  [exchange(): both = lax.all_gather(sent, FRONT[1], axis=0, tiled=True)]
    pallas_call x15, Pallas kernels: 4.81 us -> 7.68 us  [call(): pl.pallas_call(body, out_shape=outs, in_specs=[whole(space)] * len(inputs...]
where the time goes in v5:
time: 176 us; the launch traced here: 175 us
  blocking collectives  168 us (95%)
  Pallas kernels  7.68 us (4%)
    all_to_all x12, blocking collectives, over(): return lax.all_to_all(value, names, 0, 0, tiled=True)  164 us
    pallas_call x15, Pallas kernels, call(): pl.pallas_call(body, out_shape=outs, in_specs=[whole(space)] * len(inputs...  7.68 us
    all_gather x2, blocking collectives, exchange(): both = lax.all_gather(sent, FRONT[1], axis=0, tiled=True)  3.65 us

profile of v5, /device:TPU:24, one launch (start us, length us, event | category | flops | bytes accessed | tf_op | source)
XLA Modules:
  0.0 175.3 jit_solution(5835221524641911754)
XLA Ops:
  0.0 2.5 %shard_map.46 = (bf16[8,3,4,120]{3,2,1,0:T(4,128)(2,1)S(1)}, f32[5,2,16,40]{3,2,1,0:T(8,128)S(1)}, bf16[2,320,2480]{2,1,0:T(8,128)(2,1)S(1)}, bf16[2,320,1200]{2,1,0:T(8,128)(2,1)S(1)}, s32[1,30]{1,0:T(1,128)S(1)}) custom-call(f32[5,2,16,40]{3,2,1,0:T(8,128)} %rhs_hbm.1, bf16[2,320,2480]{2,1,0:T(8,128)(2,1)} %inv_hbm.1, bf16[2,320,1200]{2,1,0:T(8,128)(2,1)} %upd_hbm.1, ...), custom_call_target="tpu_custom_call" | custom-call | tf_op jit(solution)/shard_map/pallas_call | solution.py:27
  2.5 9.5 %all_to_all.60.received_ref = bf16[8,3,4,120]{3,2,1,0:T(4,128)(2,1)S(1)} all-to-all(bf16[8,3,4,120]{3,2,1,0:T(4,128)(2,1)S(1)} %get-tuple-element.19), channel_id=1, replica_groups=mesh['y1'=2,'y0'=2,'z3'=2,'z2'=2,'z1'=2,'z0'=2,'x'=4,'core'=2] {'x','core'}, dimensions={0} | all-to-all | bytes 46080 | tf_op jit(solution)/shard_map/all_to_all | solution.py:134
  12.0 0.4 shard_map.47
  12.4 9.8 %all_to_all.61.received_ref = bf16[16,3,4,120]{3,2,1,0:T(4,128)(2,1)S(1)} all-to-all(bf16[16,3,4,120]{3,2,1,0:T(4,128)(2,1)S(1)} %shard_map.47), channel_id=1, replica_groups=mesh['y1'=2,'y0'=2,'z3'=2,'z2'=2,'z1'=2,'z0'=2,'x'=4,'core'=2] {'z0','x'..., dimensions={0} | all-to-all | bytes 92160 | tf_op jit(solution)/shard_map/all_to_all | solution.py:134
  22.2 0.5 shard_map.48
  22.7 8.7 %all_to_all.62.received_ref = bf16[16,3,4,120]{3,2,1,0:T(4,128)(2,1)S(1)} all-to-all(bf16[16,3,4,120]{3,2,1,0:T(4,128)(2,1)S(1)} %get-tuple-element.23), channel_id=1, replica_groups=mesh['y1'=2,'y0'=2,'z3'=2,'z2'=2,'z1'=2,'z0'=2,'x'=4,'core'=2] {'z0','x'..., dimensions={0} | all-to-all | bytes 92160 | tf_op jit(solution)/shard_map/all_to_all | solution.py:134
  31.3 0.4 shard_map.49
  31.7 13.6 %all_to_all.63.received_ref = bf16[32,3,4,120]{3,2,1,0:T(4,128)(2,1)S(1)} all-to-all(bf16[32,3,4,120]{3,2,1,0:T(4,128)(2,1)S(1)} %shard_map.49), channel_id=1, replica_groups=mesh['y1'=2,'y0'=2,'z3'=2,'z2'=2,'z1'=2,'z0'=2,'x'=4,'core'=2] {'z1','z0..., dimensions={0} | all-to-all | bytes 184320 | tf_op jit(solution)/shard_map/all_to_all | solution.py:134
  45.4 0.5 shard_map.50
  45.9 11.5 %all_to_all.64.received_ref = bf16[32,3,4,120]{3,2,1,0:T(4,128)(2,1)S(1)} all-to-all(bf16[32,3,4,120]{3,2,1,0:T(4,128)(2,1)S(1)} %get-tuple-element.24), channel_id=1, replica_groups=mesh['y1'=2,'y0'=2,'z3'=2,'z2'=2,'z1'=2,'z0'=2,'x'=4,'core'=2] {'z1','z0..., dimensions={0} | all-to-all | bytes 184320 | tf_op jit(solution)/shard_map/all_to_all | solution.py:134
  57.4 0.4 shard_map.51
  57.9 23.2 %all_to_all.65.received_ref = bf16[32,3,4,120]{3,2,1,0:T(4,128)(2,1)S(1)} all-to-all(bf16[32,3,4,120]{3,2,1,0:T(4,128)(2,1)S(1)} %shard_map.51), channel_id=1, replica_groups=mesh['y1'=2,'y0'=2,'z3'=2,'z2'=2,'z1'=2,'z0'=2,'x'=4,'core'=2] {'z2','z1..., dimensions={0} | all-to-all | bytes 184320 | tf_op jit(solution)/shard_map/all_to_all | solution.py:134
  81.1 0.1 shard_map.52
  81.2 1.8 %all_gather.6.received_ref = bf16[8,3,4,120]{3,2,1,0:T(4,128)(2,1)S(1)} all-gather(bf16[4,3,4,120]{3,2,1,0:T(4,128)(2,1)S(1)} %get-tuple-element.25), channel_id=1, replica_groups=mesh['y1'=2,'y0'=2,'z3'=2,'z2'=2,'z1'=2,'z0'=2,'x'=4,'core'=2] {'core'}, dimensions={0}, use_global_device_ids=true | all-gather | bytes 34560 | tf_op jit(solution)/shard_map/all_gather | solution.py:225
  83.0 0.5 shard_map.53
  83.5 18.0 %all_to_all.66.received_ref = bf16[32,3,4,120]{3,2,1,0:T(4,128)(2,1)S(1)} all-to-all(bf16[32,3,4,120]{3,2,1,0:T(4,128)(2,1)S(1)} %shard_map.53), channel_id=1, replica_groups=mesh['y1'=2,'y0'=2,'z3'=2,'z2'=2,'z1'=2,'z0'=2,'x'=4,'core'=2] {'z2','z1..., dimensions={0} | all-to-all | bytes 184320 | tf_op jit(solution)/shard_map/all_to_all | solution.py:134
  101.6 1.8 %all_gather.7.received_ref = bf16[8,3,4,120]{3,2,1,0:T(4,128)(2,1)S(1)} all-gather(bf16[4,3,4,120]{3,2,1,0:T(4,128)(2,1)S(1)} %shard_map.54), channel_id=1, replica_groups=mesh['y1'=2,'y0'=2,'z3'=2,'z2'=2,'z1'=2,'z0'=2,'x'=4,'core'=2] {'core'}, dimensions={0}, use_global_device_ids=true | all-gather | bytes 34560 | tf_op jit(solution)/shard_map/all_gather | solution.py:225
  103.5 0.4 shard_map.55
  103.9 20.1 %all_to_all.67.received_ref = bf16[16,3,4,120]{3,2,1,0:T(4,128)(2,1)S(1)} all-to-all(bf16[16,3,4,120]{3,2,1,0:T(4,128)(2,1)S(1)} %shard_map.55), channel_id=1, replica_groups=mesh['y1'=2,'y0'=2,'z3'=2,'z2'=2,'z1'=2,'z0'=2,'x'=4,'core'=2] {'z3','z2..., dimensions={0} | all-to-all | bytes 92160 | tf_op jit(solution)/shard_map/all_to_all | solution.py:134
  124.0 0.1 shard_map.56
  124.1 7.9 %all_to_all.68.received_ref = bf16[8,3,4,120]{3,2,1,0:T(4,128)(2,1)S(1)} all-to-all(bf16[8,3,4,120]{3,2,1,0:T(4,128)(2,1)S(1)} %get-tuple-element.26), channel_id=1, replica_groups=mesh['y1'=2,'y0'=2,'z3'=2,'z2'=2,'z1'=2,'z0'=2,'x'=4,'core'=2] {'x','core'}, dimensions={0} | all-to-all | bytes 46080 | tf_op jit(solution)/shard_map/all_to_all | solution.py:134
  132.0 0.5 shard_map.57
  132.6 15.2 %all_to_all.69.received_ref = bf16[16,3,4,120]{3,2,1,0:T(4,128)(2,1)S(1)} all-to-all(bf16[16,3,4,120]{3,2,1,0:T(4,128)(2,1)S(1)} %shard_map.57), channel_id=1, replica_groups=mesh['y1'=2,'y0'=2,'z3'=2,'z2'=2,'z1'=2,'z0'=2,'x'=4,'core'=2] {'z3','z2..., dimensions={0} | all-to-all | bytes 92160 | tf_op jit(solution)/shard_map/all_to_all | solution.py:134
  147.8 7.8 %all_to_all.70.received_ref = bf16[8,3,4,120]{3,2,1,0:T(4,128)(2,1)S(1)} all-to-all(bf16[8,3,4,120]{3,2,1,0:T(4,128)(2,1)S(1)} %shard_map.58), channel_id=1, replica_groups=mesh['y1'=2,'y0'=2,'z3'=2,'z2'=2,'z1'=2,'z0'=2,'x'=4,'core'=2] {'x','core'}, dimensions={0} | all-to-all | bytes 46080 | tf_op jit(solution)/shard_map/all_to_all | solution.py:134
  155.6 0.6 shard_map.59
  156.1 18.5 %all_to_all.71.received_ref = bf16[32,3,4,120]{3,2,1,0:T(4,128)(2,1)S(1)} all-to-all(bf16[32,3,4,120]{3,2,1,0:T(4,128)(2,1)S(1)} %shard_map.59), channel_id=1, replica_groups=mesh['y1'=2,'y0'=2,'z3'=2,'z2'=2,'z1'=2,'z0'=2,'x'=4,'core'=2] {'y0','z3..., dimensions={0} | all-to-all | bytes 184320 | tf_op jit(solution)/shard_map/all_to_all | solution.py:134
  174.6 0.8 shard_map.60
  (2 shorter events, 0.1 us)

commit v6 on v5

--- a/solution.py
+++ b/solution.py
@@ -23,13 +23,14 @@
     return pl.BlockSpec(memory_space=space)
 
 
-def call(body, outs, inputs, space=pltpu.VMEM, scratch=()):
+def call(body, outs, inputs, space=pltpu.VMEM, scratch=(), cost=None):
     return pl.pallas_call(
         body,
         out_shape=outs,
         in_specs=[whole(space)] * len(inputs),
         out_specs=jax.tree.map(lambda _: whole(), outs),
         scratch_shapes=scratch,
+        cost_estimate=cost,
         compiler_params=pltpu.CompilerParams(vmem_limit_bytes=16 * 2**20),
     )(*inputs)
 
@@ -139,25 +140,22 @@
     def copies_of(way):
         return {WITH_FRONT: fronts, WITH_X_THEN_CORE: axes["x"], THEN_FRONT: 1}[way]
 
-    def first_body(rhs_hbm, inv_hbm, upd_hbm, mask_hbm, sent, rhs_ref, inverse, upd, mask, sems):
-        pairs = ((rhs_hbm, rhs_ref), (inv_hbm, inverse), (upd_hbm, upd), (mask_hbm, mask))
-        moves = [pltpu.make_async_copy(a, b, sems.at[k]) for k, (a, b) in enumerate(pairs)]
-        for move in moves:
-            move.start()
-        moves[0].wait()
+    def first_body(rhs_hbm, sent, rhs_ref, sem):
+        move = pltpu.make_async_copy(rhs_hbm, rhs_ref, sem)
+        move.start()
+        move.wait()
         put(sent, range(fronts), packing.pack(both_parts(rhs_ref, levels - 1)))
-        for move in moves[1:]:
-            move.wait()
 
     def same(array):
         return jax.ShapeDtypeStruct(array.shape, array.dtype)
 
-    sent, rhs, inv_blocks, upd_blocks, tile_mask = call(
+    sent, rhs = call(
         first_body,
-        (sent_shape(fronts), same(rhs), same(inv_blocks), same(upd_blocks), same(tile_mask)),
-        [pltpu.with_memory_space_constraint(a, pltpu.HBM) for a in (rhs, inv_blocks, upd_blocks, tile_mask)],
+        (sent_shape(fronts), same(rhs)),
+        (pltpu.with_memory_space_constraint(rhs, pltpu.HBM),),
         pltpu.HBM,
-        (pltpu.SemaphoreType.DMA((4,)),),
+        (pltpu.SemaphoreType.DMA(()),),
+        pl.CostEstimate(flops=10**10, transcendentals=0, bytes_accessed=2 * 10**7),
     )
 
     def invert(level, received, order):

time: 176 us -> 175 us (level)
  no operation moved by 1% of the time
where the time goes in v6:
time: 175 us; the launch traced here: 174 us
  blocking collectives  168 us (96%)
  Pallas kernels  6.29 us (4%)
    all_to_all x12, blocking collectives, over(): return lax.all_to_all(value, names, 0, 0, tiled=True)  164 us
    pallas_call x15, Pallas kernels, call(): pl.pallas_call(body, out_shape=outs, in_specs=[whole(space)] * len(inputs...  6.29 us
    all_gather x2, blocking collectives, exchange(): both = lax.all_gather(sent, FRONT[1], axis=0, tiled=True)  3.65 us

profile of v6, /device:TPU:24, one launch (start us, length us, event | category | flops | bytes accessed | tf_op | source)
XLA Modules:
  0.0 174.1 jit_solution(15400071591738786239)
XLA Ops:
  0.0 0.0 copy-start
  0.0 1.1 shard_map.46
  1.1 0.0 copy-start.1
  1.1 0.0 copy-start.2
  1.2 9.6 %all_to_all.60.received_ref = bf16[8,3,4,120]{3,2,1,0:T(4,128)(2,1)S(1)} all-to-all(bf16[8,3,4,120]{3,2,1,0:T(4,128)(2,1)S(1)} %get-tuple-element.15), channel_id=1, replica_groups=mesh['y1'=2,'y0'=2,'z3'=2,'z2'=2,'z1'=2,'z0'=2,'x'=4,'core'=2] {'x','core'}, dimensions={0} | all-to-all | bytes 46080 | tf_op jit(solution)/shard_map/all_to_all | solution.py:135
  10.8 0.0 copy-done
  10.8 0.4 shard_map.47
  11.2 9.8 %all_to_all.61.received_ref = bf16[16,3,4,120]{3,2,1,0:T(4,128)(2,1)S(1)} all-to-all(bf16[16,3,4,120]{3,2,1,0:T(4,128)(2,1)S(1)} %shard_map.47), channel_id=1, replica_groups=mesh['y1'=2,'y0'=2,'z3'=2,'z2'=2,'z1'=2,'z0'=2,'x'=4,'core'=2] {'z0','x'..., dimensions={0} | all-to-all | bytes 92160 | tf_op jit(solution)/shard_map/all_to_all | solution.py:135
  21.0 0.0 copy-done.1
  21.0 0.0 copy-done.2
  21.0 0.5 shard_map.48
  21.5 8.7 %all_to_all.62.received_ref = bf16[16,3,4,120]{3,2,1,0:T(4,128)(2,1)S(1)} all-to-all(bf16[16,3,4,120]{3,2,1,0:T(4,128)(2,1)S(1)} %get-tuple-element.17), channel_id=1, replica_groups=mesh['y1'=2,'y0'=2,'z3'=2,'z2'=2,'z1'=2,'z0'=2,'x'=4,'core'=2] {'z0','x'..., dimensions={0} | all-to-all | bytes 92160 | tf_op jit(solution)/shard_map/all_to_all | solution.py:135
  30.1 0.4 shard_map.49
  30.5 13.6 %all_to_all.63.received_ref = bf16[32,3,4,120]{3,2,1,0:T(4,128)(2,1)S(1)} all-to-all(bf16[32,3,4,120]{3,2,1,0:T(4,128)(2,1)S(1)} %shard_map.49), channel_id=1, replica_groups=mesh['y1'=2,'y0'=2,'z3'=2,'z2'=2,'z1'=2,'z0'=2,'x'=4,'core'=2] {'z1','z0..., dimensions={0} | all-to-all | bytes 184320 | tf_op jit(solution)/shard_map/all_to_all | solution.py:135
  44.2 0.5 shard_map.50
  44.6 11.5 %all_to_all.64.received_ref = bf16[32,3,4,120]{3,2,1,0:T(4,128)(2,1)S(1)} all-to-all(bf16[32,3,4,120]{3,2,1,0:T(4,128)(2,1)S(1)} %get-tuple-element.18), channel_id=1, replica_groups=mesh['y1'=2,'y0'=2,'z3'=2,'z2'=2,'z1'=2,'z0'=2,'x'=4,'core'=2] {'z1','z0..., dimensions={0} | all-to-all | bytes 184320 | tf_op jit(solution)/shard_map/all_to_all | solution.py:135
  56.2 0.5 shard_map.51
  56.7 23.2 %all_to_all.65.received_ref = bf16[32,3,4,120]{3,2,1,0:T(4,128)(2,1)S(1)} all-to-all(bf16[32,3,4,120]{3,2,1,0:T(4,128)(2,1)S(1)} %shard_map.51), channel_id=1, replica_groups=mesh['y1'=2,'y0'=2,'z3'=2,'z2'=2,'z1'=2,'z0'=2,'x'=4,'core'=2] {'z2','z1..., dimensions={0} | all-to-all | bytes 184320 | tf_op jit(solution)/shard_map/all_to_all | solution.py:135
  79.9 0.1 shard_map.52
  80.0 1.8 %all_gather.6.received_ref = bf16[8,3,4,120]{3,2,1,0:T(4,128)(2,1)S(1)} all-gather(bf16[4,3,4,120]{3,2,1,0:T(4,128)(2,1)S(1)} %get-tuple-element.19), channel_id=1, replica_groups=mesh['y1'=2,'y0'=2,'z3'=2,'z2'=2,'z1'=2,'z0'=2,'x'=4,'core'=2] {'core'}, dimensions={0}, use_global_device_ids=true | all-gather | bytes 34560 | tf_op jit(solution)/shard_map/all_gather | solution.py:223
  81.8 0.5 shard_map.53
  82.3 18.0 %all_to_all.66.received_ref = bf16[32,3,4,120]{3,2,1,0:T(4,128)(2,1)S(1)} all-to-all(bf16[32,3,4,120]{3,2,1,0:T(4,128)(2,1)S(1)} %shard_map.53), channel_id=1, replica_groups=mesh['y1'=2,'y0'=2,'z3'=2,'z2'=2,'z1'=2,'z0'=2,'x'=4,'core'=2] {'z2','z1..., dimensions={0} | all-to-all | bytes 184320 | tf_op jit(solution)/shard_map/all_to_all | solution.py:135
  100.4 1.8 %all_gather.7.received_ref = bf16[8,3,4,120]{3,2,1,0:T(4,128)(2,1)S(1)} all-gather(bf16[4,3,4,120]{3,2,1,0:T(4,128)(2,1)S(1)} %shard_map.54), channel_id=1, replica_groups=mesh['y1'=2,'y0'=2,'z3'=2,'z2'=2,'z1'=2,'z0'=2,'x'=4,'core'=2] {'core'}, dimensions={0}, use_global_device_ids=true | all-gather | bytes 34560 | tf_op jit(solution)/shard_map/all_gather | solution.py:223
  102.2 0.4 shard_map.55
  102.7 20.1 %all_to_all.67.received_ref = bf16[16,3,4,120]{3,2,1,0:T(4,128)(2,1)S(1)} all-to-all(bf16[16,3,4,120]{3,2,1,0:T(4,128)(2,1)S(1)} %shard_map.55), channel_id=1, replica_groups=mesh['y1'=2,'y0'=2,'z3'=2,'z2'=2,'z1'=2,'z0'=2,'x'=4,'core'=2] {'z3','z2..., dimensions={0} | all-to-all | bytes 92160 | tf_op jit(solution)/shard_map/all_to_all | solution.py:135
  122.8 0.1 shard_map.56
  122.9 7.9 %all_to_all.68.received_ref = bf16[8,3,4,120]{3,2,1,0:T(4,128)(2,1)S(1)} all-to-all(bf16[8,3,4,120]{3,2,1,0:T(4,128)(2,1)S(1)} %get-tuple-element.20), channel_id=1, replica_groups=mesh['y1'=2,'y0'=2,'z3'=2,'z2'=2,'z1'=2,'z0'=2,'x'=4,'core'=2] {'x','core'}, dimensions={0} | all-to-all | bytes 46080 | tf_op jit(solution)/shard_map/all_to_all | solution.py:135
  130.8 0.5 shard_map.57
  131.4 15.2 %all_to_all.69.received_ref = bf16[16,3,4,120]{3,2,1,0:T(4,128)(2,1)S(1)} all-to-all(bf16[16,3,4,120]{3,2,1,0:T(4,128)(2,1)S(1)} %shard_map.57), channel_id=1, replica_groups=mesh['y1'=2,'y0'=2,'z3'=2,'z2'=2,'z1'=2,'z0'=2,'x'=4,'core'=2] {'z3','z2..., dimensions={0} | all-to-all | bytes 92160 | tf_op jit(solution)/shard_map/all_to_all | solution.py:135
  146.6 7.8 %all_to_all.70.received_ref = bf16[8,3,4,120]{3,2,1,0:T(4,128)(2,1)S(1)} all-to-all(bf16[8,3,4,120]{3,2,1,0:T(4,128)(2,1)S(1)} %shard_map.58), channel_id=1, replica_groups=mesh['y1'=2,'y0'=2,'z3'=2,'z2'=2,'z1'=2,'z0'=2,'x'=4,'core'=2] {'x','core'}, dimensions={0} | all-to-all | bytes 46080 | tf_op jit(solution)/shard_map/all_to_all | solution.py:135
  154.3 0.6 shard_map.59
  154.9 18.5 %all_to_all.71.received_ref = bf16[32,3,4,120]{3,2,1,0:T(4,128)(2,1)S(1)} all-to-all(bf16[32,3,4,120]{3,2,1,0:T(4,128)(2,1)S(1)} %shard_map.59), channel_id=1, replica_groups=mesh['y1'=2,'y0'=2,'z3'=2,'z2'=2,'z1'=2,'z0'=2,'x'=4,'core'=2] {'y0','z3..., dimensions={0} | all-to-all | bytes 184320 | tf_op jit(solution)/shard_map/all_to_all | solution.py:135
  173.3 0.8 shard_map.60
  (2 shorter events, 0.1 us)
Async XLA Ops:
  0.0 10.8 %copy-start = (bf16[2,320,2480]{2,1,0:T(8,128)(2,1)S(1)}, bf16[2,320,2480]{2,1,0:T(8,128)(2,1)}, u32[]{:S(2)}) copy-start(bf16[2,320,2480]{2,1,0:T(8,128)(2,1)} %matrix.17) | copy-start | bytes 9523204
  1.1 19.9 %copy-start.1 = (bf16[2,320,1200]{2,1,0:T(8,128)(2,1)S(1)}, bf16[2,320,1200]{2,1,0:T(8,128)(2,1)}, u32[]{:S(2)}) copy-start(bf16[2,320,1200]{2,1,0:T(8,128)(2,1)} %matrix.16) | copy-start | bytes 4608004
  1.1 19.8 %copy-start.2 = (s32[1,30]{1,0:T(1,128)S(1)}, s32[1,30]{1,0:T(1,128)}, u32[]{:S(2)}) copy-start(s32[1,30]{1,0:T(1,128)} %mask.7) | copy-start | bytes 364

commit v7 on v6

--- a/solution.py
+++ b/solution.py
@@ -10,6 +10,13 @@
 FRONT = ("x", "core")
 WITH_FRONT, THEN_FRONT, WITH_X_THEN_CORE = range(3)
 WAY = {4: WITH_FRONT, 3: WITH_FRONT, 2: WITH_X_THEN_CORE, 1: THEN_FRONT}
+GROUP = {
+    4: ("z0", "x", "core"),
+    3: ("z0", "x", "core", "z1"),
+    2: ("z0", "x", "z1", "z2"),
+    1: ("z1", "z2", "z3", "z0"),
+    0: ("z3", "z2", "z1", "z0", "y0"),
+}
 STRIP = 4
 
 
@@ -134,11 +141,28 @@
     def over(value, names):
         return lax.all_to_all(value, names, 0, 0, tiled=True)
 
-    def by_front(count):
-        return [[m * fronts + c for m in range(count)] for c in range(fronts)]
-
-    def copies_of(way):
-        return {WITH_FRONT: fronts, WITH_X_THEN_CORE: axes["x"], THEN_FRONT: 1}[way]
+    def slot(names, member, x=0, core=0):
+        place = 0
+        for name in names:
+            if name in FRONT:
+                here = x if name == "x" else core
+            else:
+                here = member >> LEAF[::-1].index(name) & 1
+            place = place * axes[name] + here
+        return place
+
+    def by_front(names, count):
+        pairs = [(x, core) for x in range(axes["x"]) for core in range(axes["core"])]
+        return [[slot(names, m, *pair) for m in range(count)] for pair in pairs]
+
+    def member_slots(level, member):
+        names = GROUP[level]
+        xs = range(axes["x"] if "x" in names else 1)
+        cores = range(axes["core"] if "core" in names else 1)
+        return [slot(names, member, x, core) for x in xs for core in cores]
+
+    def message_count(level):
+        return len(member_slots(level, 0)) * (blocks >> (level + 1))
 
     def first_body(rhs_hbm, sent, rhs_ref, sem):
         move = pltpu.make_async_copy(rhs_hbm, rhs_ref, sem)
@@ -160,7 +184,6 @@
 
     def invert(level, received, order):
         members = blocks >> (level + 1)
-        copies = copies_of(WAY[level]) if level > 0 else 1
 
         def body(received_ref, matrix, sent):
             block = packing.unpack(summed_chunks(received_ref, order))
@@ -168,13 +191,12 @@
             for a in range(members):
                 lane = shift + a * rows_dev
                 strips = packing.pack(out[:, lane : lane + rows_dev])
-                put(sent, range(a * copies, (a + 1) * copies), strips)
-
-        return call(body, sent_shape(members * copies), (received, inv_blocks))
+                put(sent, member_slots(level, a), strips)
+
+        return call(body, sent_shape(message_count(level)), (received, inv_blocks))
 
     def update(level, received, order, known):
         members = blocks >> (level + 1)
-        copies = copies_of(WAY[level])
         offset = blocks // 2 - 2 * members
 
         def body(mask, received_ref, rhs_ref, matrix, *outs):
@@ -190,18 +212,18 @@
                 lane = shift + a * rows_dev
                 part = out[:, lane : lane + rows_dev] * gates[:, offset + a : offset + a + 1]
                 strips = packing.pack(jnp.where(own == a, right, 0.0) - part)
-                put(sent, range(a * copies, (a + 1) * copies), strips)
-
-        outs = (sent_shape(members * copies),) + (() if known else (sol_shape,))
+                put(sent, member_slots(level, a), strips)
+
+        outs = (sent_shape(message_count(level)),) + (() if known else (sol_shape,))
         return call(body, outs, (tile_mask, received, rhs, upd_blocks))
 
     def combine(level, received, solution):
         members = blocks >> (level + 1)
-        kept = copies_of(WAY[level])
+        kept = axes["x"] if "x" in GROUP[level] else 1
         copies = fronts if WAY[level] == THEN_FRONT else 1
 
         def body(received_ref, sent, *outs):
-            chunks = summed_chunks(received_ref, [[m * kept + k for m in range(members)] for k in range(kept)])
+            chunks = summed_chunks(received_ref, [[slot(GROUP[level], m, k) for m in range(members)] for k in range(kept)])
             if solution:
                 own = lax.axis_index("x") if kept > 1 else 0
                 write_solution(outs[0], own_chunk(chunks, own))
@@ -212,17 +234,14 @@
         return call(body, outs, (received,))
 
     def exchange(level, sent, solution):
-        members = blocks >> (level + 1)
-        group = LEAF[len(LEAF) - (levels - level) :]
+        names = GROUP[level]
         if WAY[level] == WITH_FRONT:
-            return over(sent, group + FRONT), by_front(members), None
+            return over(sent, names), by_front(names, blocks >> (level + 1)), None
+        sent, *solved = combine(level, over(sent, names), solution)
         if WAY[level] == THEN_FRONT:
-            sent, *solved = combine(level, over(sent, group), solution)
-            return over(sent, FRONT), by_front(1), solved[0] if solution else None
-        sent, *solved = combine(level, over(sent, group + FRONT[:1]), solution)
-        both = lax.all_gather(sent, FRONT[1], axis=0, tiled=True)
-        order = [[(c % axes["core"]) * axes["x"] + c // axes["core"]] for c in range(fronts)]
-        return both, order, solved[0] if solution else None
+            return over(sent, FRONT), by_front(FRONT, 1), solved[0] if solution else None
+        both = lax.all_gather(sent, "core", axis=0, tiled=True)
+        return both, by_front(("core", "x"), 1), solved[0] if solution else None
 
     def finish(received, solved):
         def body(received_ref, *refs):
@@ -233,7 +252,7 @@
 
         return call(body, same(rhs), (received, *solved))
 
-    received, order = over(sent, FRONT), by_front(1)
+    received, order = over(sent, FRONT), by_front(FRONT, 1)
     solved = [None] * levels
     for level in range(levels - 1, 0, -1):
         received, order, solved[level] = exchange(level, invert(level, received, order), True)
@@ -241,7 +260,7 @@
         if rest:
             solved[level] = rest[0]
         received, order, _ = exchange(level, sent, False)
-    return finish(over(invert(0, received, order), LEAF[1:]), solved[1:])
+    return finish(over(invert(0, received, order), GROUP[0]), solved[1:])
 
 
 def solution(mesh):

time: 175 us -> 175 us (level)
  no operation moved by 1% of the time
where the time goes in v7:
time: 175 us; the launch traced here: 174 us
  blocking collectives  168 us (96%)
  Pallas kernels  6.29 us (4%)
    all_to_all x12, blocking collectives, over(): return lax.all_to_all(value, names, 0, 0, tiled=True)  164 us
    pallas_call x15, Pallas kernels, call(): pl.pallas_call(body, out_shape=outs, in_specs=[whole(space)] * len(inputs...  6.29 us
    all_gather x2, blocking collectives, exchange(): both = lax.all_gather(sent, 'core', axis=0, tiled=True)  3.65 us

profile of v7, /device:TPU:24, one launch (start us, length us, event | category | flops | bytes accessed | tf_op | source)
XLA Modules:
  0.0 174.2 jit_solution(11291722736581613056)
XLA Ops:
  0.0 0.0 copy-start
  0.0 1.1 shard_map.46
  1.1 0.0 copy-start.1
  1.1 0.0 copy-start.2
  1.2 9.6 %all_to_all.60.received_ref = bf16[8,3,4,120]{3,2,1,0:T(4,128)(2,1)S(1)} all-to-all(bf16[8,3,4,120]{3,2,1,0:T(4,128)(2,1)S(1)} %get-tuple-element.15), channel_id=1, replica_groups=mesh['y1'=2,'y0'=2,'z3'=2,'z2'=2,'z1'=2,'z0'=2,'x'=4,'core'=2] {'x','core'}, dimensions={0} | all-to-all | bytes 46080 | tf_op jit(solution)/shard_map/all_to_all | solution.py:142
  10.8 0.0 copy-done
  10.8 0.4 shard_map.47
  11.2 9.8 %all_to_all.61.received_ref = bf16[16,3,4,120]{3,2,1,0:T(4,128)(2,1)S(1)} all-to-all(bf16[16,3,4,120]{3,2,1,0:T(4,128)(2,1)S(1)} %shard_map.47), channel_id=1, replica_groups=mesh['y1'=2,'y0'=2,'z3'=2,'z2'=2,'z1'=2,'z0'=2,'x'=4,'core'=2] {'z0','x'..., dimensions={0} | all-to-all | bytes 92160 | tf_op jit(solution)/shard_map/all_to_all | solution.py:142
  21.0 0.0 copy-done.1
  21.0 0.0 copy-done.2
  21.0 0.5 shard_map.48
  21.5 8.7 %all_to_all.62.received_ref = bf16[16,3,4,120]{3,2,1,0:T(4,128)(2,1)S(1)} all-to-all(bf16[16,3,4,120]{3,2,1,0:T(4,128)(2,1)S(1)} %get-tuple-element.17), channel_id=1, replica_groups=mesh['y1'=2,'y0'=2,'z3'=2,'z2'=2,'z1'=2,'z0'=2,'x'=4,'core'=2] {'z0','x'..., dimensions={0} | all-to-all | bytes 92160 | tf_op jit(solution)/shard_map/all_to_all | solution.py:142
  30.1 0.4 shard_map.49
  30.5 13.8 %all_to_all.63.received_ref = bf16[32,3,4,120]{3,2,1,0:T(4,128)(2,1)S(1)} all-to-all(bf16[32,3,4,120]{3,2,1,0:T(4,128)(2,1)S(1)} %shard_map.49), channel_id=1, replica_groups=mesh['y1'=2,'y0'=2,'z3'=2,'z2'=2,'z1'=2,'z0'=2,'x'=4,'core'=2] {'z0','x'..., dimensions={0} | all-to-all | bytes 184320 | tf_op jit(solution)/shard_map/all_to_all | solution.py:142
  44.4 0.5 shard_map.50
  44.8 11.4 %all_to_all.64.received_ref = bf16[32,3,4,120]{3,2,1,0:T(4,128)(2,1)S(1)} all-to-all(bf16[32,3,4,120]{3,2,1,0:T(4,128)(2,1)S(1)} %get-tuple-element.18), channel_id=1, replica_groups=mesh['y1'=2,'y0'=2,'z3'=2,'z2'=2,'z1'=2,'z0'=2,'x'=4,'core'=2] {'z0','x'..., dimensions={0} | all-to-all | bytes 184320 | tf_op jit(solution)/shard_map/all_to_all | solution.py:142
  56.2 0.5 shard_map.51
  56.6 23.3 %all_to_all.65.received_ref = bf16[32,3,4,120]{3,2,1,0:T(4,128)(2,1)S(1)} all-to-all(bf16[32,3,4,120]{3,2,1,0:T(4,128)(2,1)S(1)} %shard_map.51), channel_id=1, replica_groups=mesh['y1'=2,'y0'=2,'z3'=2,'z2'=2,'z1'=2,'z0'=2,'x'=4,'core'=2] {'z0','x'..., dimensions={0} | all-to-all | bytes 184320 | tf_op jit(solution)/shard_map/all_to_all | solution.py:142
  80.0 0.1 shard_map.52
  80.1 1.8 %all_gather.6.received_ref = bf16[8,3,4,120]{3,2,1,0:T(4,128)(2,1)S(1)} all-gather(bf16[4,3,4,120]{3,2,1,0:T(4,128)(2,1)S(1)} %get-tuple-element.19), channel_id=1, replica_groups=mesh['y1'=2,'y0'=2,'z3'=2,'z2'=2,'z1'=2,'z0'=2,'x'=4,'core'=2] {'core'}, dimensions={0}, use_global_device_ids=true | all-gather | bytes 34560 | tf_op jit(solution)/shard_map/all_gather | solution.py:243
  81.9 0.5 shard_map.53
  82.4 17.8 %all_to_all.66.received_ref = bf16[32,3,4,120]{3,2,1,0:T(4,128)(2,1)S(1)} all-to-all(bf16[32,3,4,120]{3,2,1,0:T(4,128)(2,1)S(1)} %shard_map.53), channel_id=1, replica_groups=mesh['y1'=2,'y0'=2,'z3'=2,'z2'=2,'z1'=2,'z0'=2,'x'=4,'core'=2] {'z0','x'..., dimensions={0} | all-to-all | bytes 184320 | tf_op jit(solution)/shard_map/all_to_all | solution.py:142
  100.3 1.8 %all_gather.7.received_ref = bf16[8,3,4,120]{3,2,1,0:T(4,128)(2,1)S(1)} all-gather(bf16[4,3,4,120]{3,2,1,0:T(4,128)(2,1)S(1)} %shard_map.54), channel_id=1, replica_groups=mesh['y1'=2,'y0'=2,'z3'=2,'z2'=2,'z1'=2,'z0'=2,'x'=4,'core'=2] {'core'}, dimensions={0}, use_global_device_ids=true | all-gather | bytes 34560 | tf_op jit(solution)/shard_map/all_gather | solution.py:243
  102.1 0.4 shard_map.55
  102.5 20.4 %all_to_all.67.received_ref = bf16[16,3,4,120]{3,2,1,0:T(4,128)(2,1)S(1)} all-to-all(bf16[16,3,4,120]{3,2,1,0:T(4,128)(2,1)S(1)} %shard_map.55), channel_id=1, replica_groups=mesh['y1'=2,'y0'=2,'z3'=2,'z2'=2,'z1'=2,'z0'=2,'x'=4,'core'=2] {'z1','z2..., dimensions={0} | all-to-all | bytes 92160 | tf_op jit(solution)/shard_map/all_to_all | solution.py:142
  123.0 0.1 shard_map.56
  123.0 7.8 %all_to_all.68.received_ref = bf16[8,3,4,120]{3,2,1,0:T(4,128)(2,1)S(1)} all-to-all(bf16[8,3,4,120]{3,2,1,0:T(4,128)(2,1)S(1)} %get-tuple-element.20), channel_id=1, replica_groups=mesh['y1'=2,'y0'=2,'z3'=2,'z2'=2,'z1'=2,'z0'=2,'x'=4,'core'=2] {'x','core'}, dimensions={0} | all-to-all | bytes 46080 | tf_op jit(solution)/shard_map/all_to_all | solution.py:142
  130.8 0.5 shard_map.57
  131.3 15.1 %all_to_all.69.received_ref = bf16[16,3,4,120]{3,2,1,0:T(4,128)(2,1)S(1)} all-to-all(bf16[16,3,4,120]{3,2,1,0:T(4,128)(2,1)S(1)} %shard_map.57), channel_id=1, replica_groups=mesh['y1'=2,'y0'=2,'z3'=2,'z2'=2,'z1'=2,'z0'=2,'x'=4,'core'=2] {'z1','z2..., dimensions={0} | all-to-all | bytes 92160 | tf_op jit(solution)/shard_map/all_to_all | solution.py:142
  146.5 7.8 %all_to_all.70.received_ref = bf16[8,3,4,120]{3,2,1,0:T(4,128)(2,1)S(1)} all-to-all(bf16[8,3,4,120]{3,2,1,0:T(4,128)(2,1)S(1)} %shard_map.58), channel_id=1, replica_groups=mesh['y1'=2,'y0'=2,'z3'=2,'z2'=2,'z1'=2,'z0'=2,'x'=4,'core'=2] {'x','core'}, dimensions={0} | all-to-all | bytes 46080 | tf_op jit(solution)/shard_map/all_to_all | solution.py:142
  154.3 0.6 shard_map.59
  154.8 18.6 %all_to_all.71.received_ref = bf16[32,3,4,120]{3,2,1,0:T(4,128)(2,1)S(1)} all-to-all(bf16[32,3,4,120]{3,2,1,0:T(4,128)(2,1)S(1)} %shard_map.59), channel_id=1, replica_groups=mesh['y1'=2,'y0'=2,'z3'=2,'z2'=2,'z1'=2,'z0'=2,'x'=4,'core'=2] {'z3','z2..., dimensions={0} | all-to-all | bytes 184320 | tf_op jit(solution)/shard_map/all_to_all | solution.py:142
  173.4 0.8 shard_map.60
  (2 shorter events, 0.1 us)
Async XLA Ops:
  0.0 10.8 %copy-start = (bf16[2,320,2480]{2,1,0:T(8,128)(2,1)S(1)}, bf16[2,320,2480]{2,1,0:T(8,128)(2,1)}, u32[]{:S(2)}) copy-start(bf16[2,320,2480]{2,1,0:T(8,128)(2,1)} %matrix.17) | copy-start | bytes 9523204
  1.1 19.9 %copy-start.1 = (bf16[2,320,1200]{2,1,0:T(8,128)(2,1)S(1)}, bf16[2,320,1200]{2,1,0:T(8,128)(2,1)}, u32[]{:S(2)}) copy-start(bf16[2,320,1200]{2,1,0:T(8,128)(2,1)} %matrix.16) | copy-start | bytes 4608004
  1.1 19.8 %copy-start.2 = (s32[1,30]{1,0:T(1,128)S(1)}, s32[1,30]{1,0:T(1,128)}, u32[]{:S(2)}) copy-start(s32[1,30]{1,0:T(1,128)} %mask.7) | copy-start | bytes 364

commit v8 on v7

--- a/solution.py
+++ b/solution.py
@@ -9,15 +9,15 @@
 LEAF = ("y1", "y0", "z3", "z2", "z1", "z0")
 FRONT = ("x", "core")
 WITH_FRONT, THEN_FRONT, WITH_X_THEN_CORE = range(3)
-WAY = {4: WITH_FRONT, 3: WITH_FRONT, 2: WITH_X_THEN_CORE, 1: THEN_FRONT}
+WAY = {4: WITH_FRONT, 3: WITH_FRONT, 2: WITH_X_THEN_CORE, 1: WITH_X_THEN_CORE}
 GROUP = {
     4: ("z0", "x", "core"),
     3: ("z0", "x", "core", "z1"),
     2: ("z0", "x", "z1", "z2"),
-    1: ("z1", "z2", "z3", "z0"),
+    1: ("z0", "z1", "z2", "z3", "x"),
     0: ("z3", "z2", "z1", "z0", "y0"),
 }
-STRIP = 4
+STRIP = 2
 
 
 def lane_window(columns, start, width):
@@ -44,35 +44,32 @@
 
 class Packing:
     def __init__(self, rows, lanes):
-        self.rows, self.lanes = rows, lanes
+        self.lanes = lanes
+        self.depth = rows * lanes // 128
         self.groups = 128 // lanes
-        self.strips = -(-rows // (self.groups * STRIP))
-        self.shape = (self.strips, STRIP, self.groups * lanes)
-
-    def first_row(self, group, strip):
-        return (group * self.strips + strip) * STRIP
+        self.left = 128 - self.groups * lanes
+        self.rest = rows - self.groups * self.depth
+        self.units = lanes // self.left
+        assert rows * lanes == self.depth * 128 and self.rest * self.units == self.depth
+        self.shape = (self.depth // STRIP, STRIP, 128)
 
     def pack(self, block):
-        strips = []
-        for j in range(self.strips):
-            pieces = []
-            for g in range(self.groups):
-                row = self.first_row(g, j)
-                if row < self.rows:
-                    pieces.append(block[row : row + STRIP])
-                else:
-                    pieces.append(jnp.zeros((STRIP, self.lanes), jnp.float32))
-            strips.append(jnp.concatenate(pieces, axis=1))
-        return strips
+        top = self.groups * self.depth
+        pieces = [block[g * self.depth : (g + 1) * self.depth] for g in range(self.groups)]
+        tail = [block[top:, u * self.left : (u + 1) * self.left] for u in range(self.units)]
+        packed = jnp.concatenate([*pieces, jnp.concatenate(tail, axis=0)], axis=1)
+        packed = packed.astype(jnp.bfloat16)
+        return [packed[k : k + STRIP] for k in range(0, self.depth, STRIP)]
 
     def unpack(self, chunks):
+        full = [jnp.concatenate(strips, axis=0) for strips in chunks]
         rows = []
         for g in range(self.groups):
-            for j in range(self.strips):
-                if self.first_row(g, j) < self.rows:
-                    low = g * self.lanes
-                    rows.append(jnp.concatenate([c[j][:, low : low + self.lanes] for c in chunks], axis=1))
-        return jnp.concatenate(rows, axis=0)
+            low = g * self.lanes
+            rows.append(jnp.concatenate([f[:, low : low + self.lanes] for f in full], axis=1))
+        low = self.groups * self.lanes
+        tail = [f[u * self.rest : (u + 1) * self.rest, low:] for f in full for u in range(self.units)]
+        return jnp.concatenate([*rows, jnp.concatenate(tail, axis=1)], axis=0)
 
 
 def summed_chunks(received, order):

time: 175 us -> 179 us (1.023)
  blocking collectives: 168 us -> 170 us
  Pallas kernels: 6.29 us -> 8.15 us
    all_gather x2 -> x4, blocking collectives: 3.65 us -> 7.3 us  [exchange(): both = lax.all_gather(sent, 'core', axis=0, tiled=True)]
    pallas_call x15, Pallas kernels: 6.29 us -> 8.15 us  [call(): pl.pallas_call(body, out_shape=outs, in_specs=[whole(space)] * len(inputs...]
    all_to_all x12 -> x10, blocking collectives: 164 us -> 162 us  [over(): return lax.all_to_all(value, names, 0, 0, tiled=True)]
where the time goes in v8:
time: 179 us; the launch traced here: 178 us
  blocking collectives  170 us (95%)
  Pallas kernels  8.15 us (5%)
    all_to_all x10, blocking collectives, over(): return lax.all_to_all(value, names, 0, 0, tiled=True)  162 us
    pallas_call x15, Pallas kernels, call(): pl.pallas_call(body, out_shape=outs, in_specs=[whole(space)] * len(inputs...  8.15 us
    all_gather x4, blocking collectives, exchange(): both = lax.all_gather(sent, 'core', axis=0, tiled=True)  7.3 us

profile of v8, /device:TPU:24, one launch (start us, length us, event | category | flops | bytes accessed | tf_op | source)
XLA Modules:
  0.0 178.1 jit_solution(2964804800843237924)
XLA Ops:
  0.0 0.0 copy-start
  0.0 1.2 shard_map.46
  1.2 0.0 copy-start.1
  1.2 0.0 copy-start.2
  1.2 9.6 %all_to_all.50.received_ref = bf16[8,5,2,128]{3,2,1,0:T(2,128)(2,1)S(1)} all-to-all(bf16[8,5,2,128]{3,2,1,0:T(2,128)(2,1)S(1)} %get-tuple-element.15), channel_id=1, replica_groups=mesh['y1'=2,'y0'=2,'z3'=2,'z2'=2,'z1'=2,'z0'=2,'x'=4,'core'=2] {'x','core'}, dimensions={0} | all-to-all | bytes 40960 | tf_op jit(solution)/shard_map/all_to_all | solution.py:139
  10.8 0.0 copy-done
  10.8 0.5 shard_map.47
  11.3 9.8 %all_to_all.51.received_ref = bf16[16,5,2,128]{3,2,1,0:T(2,128)(2,1)S(1)} all-to-all(bf16[16,5,2,128]{3,2,1,0:T(2,128)(2,1)S(1)} %shard_map.47), channel_id=1, replica_groups=mesh['y1'=2,'y0'=2,'z3'=2,'z2'=2,'z1'=2,'z0'=2,'x'=4,'core'=2] {'z0','x'..., dimensions={0} | all-to-all | bytes 81920 | tf_op jit(solution)/shard_map/all_to_all | solution.py:139
  21.1 0.0 copy-done.1
  21.1 0.0 copy-done.2
  21.1 0.6 shard_map.48
  21.7 8.7 %all_to_all.52.received_ref = bf16[16,5,2,128]{3,2,1,0:T(2,128)(2,1)S(1)} all-to-all(bf16[16,5,2,128]{3,2,1,0:T(2,128)(2,1)S(1)} %get-tuple-element.17), channel_id=1, replica_groups=mesh['y1'=2,'y0'=2,'z3'=2,'z2'=2,'z1'=2,'z0'=2,'x'=4,'core'=2] {'z0','x'..., dimensions={0} | all-to-all | bytes 81920 | tf_op jit(solution)/shard_map/all_to_all | solution.py:139
  30.4 0.5 shard_map.49
  30.9 13.5 %all_to_all.53.received_ref = bf16[32,5,2,128]{3,2,1,0:T(2,128)(2,1)S(1)} all-to-all(bf16[32,5,2,128]{3,2,1,0:T(2,128)(2,1)S(1)} %shard_map.49), channel_id=1, replica_groups=mesh['y1'=2,'y0'=2,'z3'=2,'z2'=2,'z1'=2,'z0'=2,'x'=4,'core'=2] {'z0','x'..., dimensions={0} | all-to-all | bytes 163840 | tf_op jit(solution)/shard_map/all_to_all | solution.py:139
  44.5 0.6 shard_map.50
  45.1 11.1 %all_to_all.54.received_ref = bf16[32,5,2,128]{3,2,1,0:T(2,128)(2,1)S(1)} all-to-all(bf16[32,5,2,128]{3,2,1,0:T(2,128)(2,1)S(1)} %get-tuple-element.18), channel_id=1, replica_groups=mesh['y1'=2,'y0'=2,'z3'=2,'z2'=2,'z1'=2,'z0'=2,'x'=4,'core'=2] {'z0','x'..., dimensions={0} | all-to-all | bytes 163840 | tf_op jit(solution)/shard_map/all_to_all | solution.py:139
  56.2 0.6 shard_map.51
  56.8 22.9 %all_to_all.55.received_ref = bf16[32,5,2,128]{3,2,1,0:T(2,128)(2,1)S(1)} all-to-all(bf16[32,5,2,128]{3,2,1,0:T(2,128)(2,1)S(1)} %shard_map.51), channel_id=1, replica_groups=mesh['y1'=2,'y0'=2,'z3'=2,'z2'=2,'z1'=2,'z0'=2,'x'=4,'core'=2] {'z0','x'..., dimensions={0} | all-to-all | bytes 163840 | tf_op jit(solution)/shard_map/all_to_all | solution.py:139
  79.7 0.1 shard_map.52
  79.8 1.8 %all_gather.12.received_ref = bf16[8,5,2,128]{3,2,1,0:T(2,128)(2,1)S(1)} all-gather(bf16[4,5,2,128]{3,2,1,0:T(2,128)(2,1)S(1)} %get-tuple-element.19), channel_id=1, replica_groups=mesh['y1'=2,'y0'=2,'z3'=2,'z2'=2,'z1'=2,'z0'=2,'x'=4,'core'=2] {'core'}, dimensions={0}, use_global_device_ids=true | all-gather | bytes 30720 | tf_op jit(solution)/shard_map/all_gather | solution.py:240
  81.6 0.7 shard_map.53
  82.3 17.2 %all_to_all.56.received_ref = bf16[32,5,2,128]{3,2,1,0:T(2,128)(2,1)S(1)} all-to-all(bf16[32,5,2,128]{3,2,1,0:T(2,128)(2,1)S(1)} %shard_map.53), channel_id=1, replica_groups=mesh['y1'=2,'y0'=2,'z3'=2,'z2'=2,'z1'=2,'z0'=2,'x'=4,'core'=2] {'z0','x'..., dimensions={0} | all-to-all | bytes 163840 | tf_op jit(solution)/shard_map/all_to_all | solution.py:139
  99.5 1.8 %all_gather.13.received_ref = bf16[8,5,2,128]{3,2,1,0:T(2,128)(2,1)S(1)} all-gather(bf16[4,5,2,128]{3,2,1,0:T(2,128)(2,1)S(1)} %shard_map.54), channel_id=1, replica_groups=mesh['y1'=2,'y0'=2,'z3'=2,'z2'=2,'z1'=2,'z0'=2,'x'=4,'core'=2] {'core'}, dimensions={0}, use_global_device_ids=true | all-gather | bytes 30720 | tf_op jit(solution)/shard_map/all_gather | solution.py:240
  101.3 0.7 shard_map.55
  102.0 28.1 %all_to_all.57.received_ref = bf16[64,5,2,128]{3,2,1,0:T(2,128)(2,1)S(1)} all-to-all(bf16[64,5,2,128]{3,2,1,0:T(2,128)(2,1)S(1)} %shard_map.55), channel_id=1, replica_groups=mesh['y1'=2,'y0'=2,'z3'=2,'z2'=2,'z1'=2,'z0'=2,'x'=4,'core'=2] {'z0','z1..., dimensions={0} | all-to-all | bytes 327680 | tf_op jit(solution)/shard_map/all_to_all | solution.py:139
  130.1 0.2 shard_map.56
  130.3 1.8 %all_gather.14.received_ref = bf16[8,5,2,128]{3,2,1,0:T(2,128)(2,1)S(1)} all-gather(bf16[4,5,2,128]{3,2,1,0:T(2,128)(2,1)S(1)} %get-tuple-element.20), channel_id=1, replica_groups=mesh['y1'=2,'y0'=2,'z3'=2,'z2'=2,'z1'=2,'z0'=2,'x'=4,'core'=2] {'core'}, dimensions={0}, use_global_device_ids=true | all-gather | bytes 30720 | tf_op jit(solution)/shard_map/all_gather | solution.py:240
  132.1 0.8 shard_map.57
  132.9 23.3 %all_to_all.58.received_ref = bf16[64,5,2,128]{3,2,1,0:T(2,128)(2,1)S(1)} all-to-all(bf16[64,5,2,128]{3,2,1,0:T(2,128)(2,1)S(1)} %shard_map.57), channel_id=1, replica_groups=mesh['y1'=2,'y0'=2,'z3'=2,'z2'=2,'z1'=2,'z0'=2,'x'=4,'core'=2] {'z0','z1..., dimensions={0} | all-to-all | bytes 327680 | tf_op jit(solution)/shard_map/all_to_all | solution.py:139
  156.2 0.1 shard_map.58
  156.3 1.8 %all_gather.15.received_ref = bf16[8,5,2,128]{3,2,1,0:T(2,128)(2,1)S(1)} all-gather(bf16[4,5,2,128]{3,2,1,0:T(2,128)(2,1)S(1)} %shard_map.58), channel_id=1, replica_groups=mesh['y1'=2,'y0'=2,'z3'=2,'z2'=2,'z1'=2,'z0'=2,'x'=4,'core'=2] {'core'}, dimensions={0}, use_global_device_ids=true | all-gather | bytes 30720 | tf_op jit(solution)/shard_map/all_gather | solution.py:240
  158.1 0.9 shard_map.59
  159.1 18.2 %all_to_all.59.received_ref = bf16[32,5,2,128]{3,2,1,0:T(2,128)(2,1)S(1)} all-to-all(bf16[32,5,2,128]{3,2,1,0:T(2,128)(2,1)S(1)} %shard_map.59), channel_id=1, replica_groups=mesh['y1'=2,'y0'=2,'z3'=2,'z2'=2,'z1'=2,'z0'=2,'x'=4,'core'=2] {'z3','z2..., dimensions={0} | all-to-all | bytes 163840 | tf_op jit(solution)/shard_map/all_to_all | solution.py:139
  177.3 0.8 shard_map.60
  (1 shorter events, 0.0 us)
Async XLA Ops:
  0.0 10.8 %copy-start = (bf16[2,320,2480]{2,1,0:T(8,128)(2,1)S(1)}, bf16[2,320,2480]{2,1,0:T(8,128)(2,1)}, u32[]{:S(2)}) copy-start(bf16[2,320,2480]{2,1,0:T(8,128)(2,1)} %matrix.17) | copy-start | bytes 9523204
  1.2 19.9 %copy-start.1 = (bf16[2,320,1200]{2,1,0:T(8,128)(2,1)S(1)}, bf16[2,320,1200]{2,1,0:T(8,128)(2,1)}, u32[]{:S(2)}) copy-start(bf16[2,320,1200]{2,1,0:T(8,128)(2,1)} %matrix.16) | copy-start | bytes 4608004
  1.2 19.9 %copy-start.2 = (s32[1,30]{1,0:T(1,128)S(1)}, s32[1,30]{1,0:T(1,128)}, u32[]{:S(2)}) copy-start(s32[1,30]{1,0:T(1,128)} %mask.7) | copy-start | bytes 364

commit v9 on v7

--- a/solution.py
+++ b/solution.py
@@ -17,6 +17,7 @@
     1: ("z1", "z2", "z3", "z0"),
     0: ("z3", "z2", "z1", "z0", "y0"),
 }
+WIRE = {4: jnp.float32, 3: jnp.float32, 2: jnp.bfloat16, 1: jnp.bfloat16, 0: jnp.bfloat16}
 STRIP = 4
 
 
@@ -111,7 +112,7 @@
 
 def put(sent, slots, strips):
     for j, strip in enumerate(strips):
-        value = strip.astype(jnp.bfloat16)
+        value = strip.astype(sent.dtype)
         for slot in slots:
             sent[slot, j] = value
 
@@ -125,8 +126,8 @@
     levels, _, rhs_count, rows_dev = rhs.shape
     packing = Packing(2 * rhs_count, rows_dev)
 
-    def sent_shape(count):
-        return jax.ShapeDtypeStruct((count,) + packing.shape, jnp.bfloat16)
+    def sent_shape(count, dtype=jnp.bfloat16):
+        return jax.ShapeDtypeStruct((count,) + packing.shape, dtype)
 
     sol_shape = jax.ShapeDtypeStruct((2, rhs_count, rows_dev), jnp.float32)
 
@@ -193,7 +194,7 @@
                 strips = packing.pack(out[:, lane : lane + rows_dev])
                 put(sent, member_slots(level, a), strips)
 
-        return call(body, sent_shape(message_count(level)), (received, inv_blocks))
+        return call(body, sent_shape(message_count(level), WIRE[level]), (received, inv_blocks))
 
     def update(level, received, order, known):
         members = blocks >> (level + 1)
@@ -214,7 +215,7 @@
                 strips = packing.pack(jnp.where(own == a, right, 0.0) - part)
                 put(sent, member_slots(level, a), strips)
 
-        outs = (sent_shape(message_count(level)),) + (() if known else (sol_shape,))
+        outs = (sent_shape(message_count(level), WIRE[level]),) + (() if known else (sol_shape,))
         return call(body, outs, (tile_mask, received, rhs, upd_blocks))
 
     def combine(level, received, solution):

time: 175 us -> 179 us (1.023)
  blocking collectives: 168 us -> 172 us
    all_to_all x12, blocking collectives: 164 us -> 168 us  [over(): return lax.all_to_all(value, names, 0, 0, tiled=True)]
where the time goes in v9:
time: 179 us; the launch traced here: 178 us
  blocking collectives  172 us (96%)
  Pallas kernels  6.29 us (4%)
    all_to_all x12, blocking collectives, over(): return lax.all_to_all(value, names, 0, 0, tiled=True)  168 us
    pallas_call x15, Pallas kernels, call(): pl.pallas_call(body, out_shape=outs, in_specs=[whole(space)] * len(inputs...  6.29 us
    all_gather x2, blocking collectives, exchange(): both = lax.all_gather(sent, 'core', axis=0, tiled=True)  3.65 us

profile of v9, /device:TPU:24, one launch (start us, length us, event | category | flops | bytes accessed | tf_op | source)
XLA Modules:
  0.0 178.3 jit_solution(7608167829947614664)
XLA Ops:
  0.0 0.0 copy-start
  0.0 1.1 shard_map.46
  1.1 0.0 copy-start.1
  1.1 0.0 copy-start.2
  1.2 9.6 %all_to_all.60.received_ref = bf16[8,3,4,120]{3,2,1,0:T(4,128)(2,1)S(1)} all-to-all(bf16[8,3,4,120]{3,2,1,0:T(4,128)(2,1)S(1)} %get-tuple-element.15), channel_id=1, replica_groups=mesh['y1'=2,'y0'=2,'z3'=2,'z2'=2,'z1'=2,'z0'=2,'x'=4,'core'=2] {'x','core'}, dimensions={0} | all-to-all | bytes 46080 | tf_op jit(solution)/shard_map/all_to_all | solution.py:143
  10.8 0.0 copy-done
  10.8 0.4 shard_map.47
  11.2 10.0 %all_to_all.61.received_ref = f32[16,3,4,120]{3,2,1,0:T(4,128)S(1)} all-to-all(f32[16,3,4,120]{3,2,1,0:T(4,128)S(1)} %shard_map.47), channel_id=1, replica_groups=mesh['y1'=2,'y0'=2,'z3'=2,'z2'=2,'z1'=2,'z0'=2,'x'=4,'core'=2] {'z0','x'..., dimensions={0} | all-to-all | bytes 184320 | tf_op jit(solution)/shard_map/all_to_all | solution.py:143
  21.2 0.0 copy-done.1
  21.2 0.0 copy-done.2
  21.2 0.5 shard_map.48
  21.7 8.9 %all_to_all.62.received_ref = f32[16,3,4,120]{3,2,1,0:T(4,128)S(1)} all-to-all(f32[16,3,4,120]{3,2,1,0:T(4,128)S(1)} %get-tuple-element.17), channel_id=1, replica_groups=mesh['y1'=2,'y0'=2,'z3'=2,'z2'=2,'z1'=2,'z0'=2,'x'=4,'core'=2] {'z0','x'..., dimensions={0} | all-to-all | bytes 184320 | tf_op jit(solution)/shard_map/all_to_all | solution.py:143
  30.5 0.4 shard_map.49
  31.0 15.3 %all_to_all.63.received_ref = f32[32,3,4,120]{3,2,1,0:T(4,128)S(1)} all-to-all(f32[32,3,4,120]{3,2,1,0:T(4,128)S(1)} %shard_map.49), channel_id=1, replica_groups=mesh['y1'=2,'y0'=2,'z3'=2,'z2'=2,'z1'=2,'z0'=2,'x'=4,'core'=2] {'z0','x'..., dimensions={0} | all-to-all | bytes 368640 | tf_op jit(solution)/shard_map/all_to_all | solution.py:143
  46.3 0.5 shard_map.50
  46.7 13.2 %all_to_all.64.received_ref = f32[32,3,4,120]{3,2,1,0:T(4,128)S(1)} all-to-all(f32[32,3,4,120]{3,2,1,0:T(4,128)S(1)} %get-tuple-element.18), channel_id=1, replica_groups=mesh['y1'=2,'y0'=2,'z3'=2,'z2'=2,'z1'=2,'z0'=2,'x'=4,'core'=2] {'z0','x'..., dimensions={0} | all-to-all | bytes 368640 | tf_op jit(solution)/shard_map/all_to_all | solution.py:143
  59.9 0.4 shard_map.51
  60.3 23.7 %all_to_all.65.received_ref = bf16[32,3,4,120]{3,2,1,0:T(4,128)(2,1)S(1)} all-to-all(bf16[32,3,4,120]{3,2,1,0:T(4,128)(2,1)S(1)} %shard_map.51), channel_id=1, replica_groups=mesh['y1'=2,'y0'=2,'z3'=2,'z2'=2,'z1'=2,'z0'=2,'x'=4,'core'=2] {'z0','x'..., dimensions={0} | all-to-all | bytes 184320 | tf_op jit(solution)/shard_map/all_to_all | solution.py:143
  84.1 0.1 shard_map.52
  84.2 1.8 %all_gather.6.received_ref = bf16[8,3,4,120]{3,2,1,0:T(4,128)(2,1)S(1)} all-gather(bf16[4,3,4,120]{3,2,1,0:T(4,128)(2,1)S(1)} %get-tuple-element.19), channel_id=1, replica_groups=mesh['y1'=2,'y0'=2,'z3'=2,'z2'=2,'z1'=2,'z0'=2,'x'=4,'core'=2] {'core'}, dimensions={0}, use_global_device_ids=true | all-gather | bytes 34560 | tf_op jit(solution)/shard_map/all_gather | solution.py:244
  86.0 0.5 shard_map.53
  86.5 17.9 %all_to_all.66.received_ref = bf16[32,3,4,120]{3,2,1,0:T(4,128)(2,1)S(1)} all-to-all(bf16[32,3,4,120]{3,2,1,0:T(4,128)(2,1)S(1)} %shard_map.53), channel_id=1, replica_groups=mesh['y1'=2,'y0'=2,'z3'=2,'z2'=2,'z1'=2,'z0'=2,'x'=4,'core'=2] {'z0','x'..., dimensions={0} | all-to-all | bytes 184320 | tf_op jit(solution)/shard_map/all_to_all | solution.py:143
  104.4 1.8 %all_gather.7.received_ref = bf16[8,3,4,120]{3,2,1,0:T(4,128)(2,1)S(1)} all-gather(bf16[4,3,4,120]{3,2,1,0:T(4,128)(2,1)S(1)} %shard_map.54), channel_id=1, replica_groups=mesh['y1'=2,'y0'=2,'z3'=2,'z2'=2,'z1'=2,'z0'=2,'x'=4,'core'=2] {'core'}, dimensions={0}, use_global_device_ids=true | all-gather | bytes 34560 | tf_op jit(solution)/shard_map/all_gather | solution.py:244
  106.2 0.4 shard_map.55
  106.7 20.4 %all_to_all.67.received_ref = bf16[16,3,4,120]{3,2,1,0:T(4,128)(2,1)S(1)} all-to-all(bf16[16,3,4,120]{3,2,1,0:T(4,128)(2,1)S(1)} %shard_map.55), channel_id=1, replica_groups=mesh['y1'=2,'y0'=2,'z3'=2,'z2'=2,'z1'=2,'z0'=2,'x'=4,'core'=2] {'z1','z2..., dimensions={0} | all-to-all | bytes 92160 | tf_op jit(solution)/shard_map/all_to_all | solution.py:143
  127.1 0.1 shard_map.56
  127.2 7.8 %all_to_all.68.received_ref = bf16[8,3,4,120]{3,2,1,0:T(4,128)(2,1)S(1)} all-to-all(bf16[8,3,4,120]{3,2,1,0:T(4,128)(2,1)S(1)} %get-tuple-element.20), channel_id=1, replica_groups=mesh['y1'=2,'y0'=2,'z3'=2,'z2'=2,'z1'=2,'z0'=2,'x'=4,'core'=2] {'x','core'}, dimensions={0} | all-to-all | bytes 46080 | tf_op jit(solution)/shard_map/all_to_all | solution.py:143
  134.9 0.5 shard_map.57
  135.5 15.1 %all_to_all.69.received_ref = bf16[16,3,4,120]{3,2,1,0:T(4,128)(2,1)S(1)} all-to-all(bf16[16,3,4,120]{3,2,1,0:T(4,128)(2,1)S(1)} %shard_map.57), channel_id=1, replica_groups=mesh['y1'=2,'y0'=2,'z3'=2,'z2'=2,'z1'=2,'z0'=2,'x'=4,'core'=2] {'z1','z2..., dimensions={0} | all-to-all | bytes 92160 | tf_op jit(solution)/shard_map/all_to_all | solution.py:143
  150.6 7.8 %all_to_all.70.received_ref = bf16[8,3,4,120]{3,2,1,0:T(4,128)(2,1)S(1)} all-to-all(bf16[8,3,4,120]{3,2,1,0:T(4,128)(2,1)S(1)} %shard_map.58), channel_id=1, replica_groups=mesh['y1'=2,'y0'=2,'z3'=2,'z2'=2,'z1'=2,'z0'=2,'x'=4,'core'=2] {'x','core'}, dimensions={0} | all-to-all | bytes 46080 | tf_op jit(solution)/shard_map/all_to_all | solution.py:143
  158.4 0.6 shard_map.59
  159.0 18.6 %all_to_all.71.received_ref = bf16[32,3,4,120]{3,2,1,0:T(4,128)(2,1)S(1)} all-to-all(bf16[32,3,4,120]{3,2,1,0:T(4,128)(2,1)S(1)} %shard_map.59), channel_id=1, replica_groups=mesh['y1'=2,'y0'=2,'z3'=2,'z2'=2,'z1'=2,'z0'=2,'x'=4,'core'=2] {'z3','z2..., dimensions={0} | all-to-all | bytes 184320 | tf_op jit(solution)/shard_map/all_to_all | solution.py:143
  177.6 0.8 shard_map.60
  (2 shorter events, 0.1 us)
Async XLA Ops:
  0.0 10.8 %copy-start = (bf16[2,320,2480]{2,1,0:T(8,128)(2,1)S(1)}, bf16[2,320,2480]{2,1,0:T(8,128)(2,1)}, u32[]{:S(2)}) copy-start(bf16[2,320,2480]{2,1,0:T(8,128)(2,1)} %matrix.17) | copy-start | bytes 9523204
  1.1 20.1 %copy-start.1 = (bf16[2,320,1200]{2,1,0:T(8,128)(2,1)S(1)}, bf16[2,320,1200]{2,1,0:T(8,128)(2,1)}, u32[]{:S(2)}) copy-start(bf16[2,320,1200]{2,1,0:T(8,128)(2,1)} %matrix.16) | copy-start | bytes 4608004
  1.1 20.0 %copy-start.2 = (s32[1,30]{1,0:T(1,128)S(1)}, s32[1,30]{1,0:T(1,128)}, u32[]{:S(2)}) copy-start(s32[1,30]{1,0:T(1,128)} %mask.7) | copy-start | bytes 364

commit v10 on v9

--- a/solution.py
+++ b/solution.py
@@ -17,7 +17,8 @@
     1: ("z1", "z2", "z3", "z0"),
     0: ("z3", "z2", "z1", "z0", "y0"),
 }
-WIRE = {4: jnp.float32, 3: jnp.float32, 2: jnp.bfloat16, 1: jnp.bfloat16, 0: jnp.bfloat16}
+WIDE_INVERSE = (4, 3)
+WIDE_UPDATE = (4,)
 STRIP = 4
 
 
@@ -126,6 +127,9 @@
     levels, _, rhs_count, rows_dev = rhs.shape
     packing = Packing(2 * rhs_count, rows_dev)
 
+    def wire(wide):
+        return jnp.float32 if wide else jnp.bfloat16
+
     def sent_shape(count, dtype=jnp.bfloat16):
         return jax.ShapeDtypeStruct((count,) + packing.shape, dtype)
 
@@ -194,7 +198,7 @@
                 strips = packing.pack(out[:, lane : lane + rows_dev])
                 put(sent, member_slots(level, a), strips)
 
-        return call(body, sent_shape(message_count(level), WIRE[level]), (received, inv_blocks))
+        return call(body, sent_shape(message_count(level), wire(level in WIDE_INVERSE)), (received, inv_blocks))
 
     def update(level, received, order, known):
         members = blocks >> (level + 1)
@@ -215,7 +219,7 @@
                 strips = packing.pack(jnp.where(own == a, right, 0.0) - part)
                 put(sent, member_slots(level, a), strips)
 
-        outs = (sent_shape(message_count(level), WIRE[level]),) + (() if known else (sol_shape,))
+        outs = (sent_shape(message_count(level), wire(level in WIDE_UPDATE)),) + (() if known else (sol_shape,))
         return call(body, outs, (tile_mask, received, rhs, upd_blocks))
 
     def combine(level, received, solution):

time: 179 us -> 177 us (0.989)
  blocking collectives: 172 us -> 170 us
    all_to_all x12, blocking collectives: 168 us -> 166 us  [over(): return lax.all_to_all(value, names, 0, 0, tiled=True)]
where the time goes in v10:
time: 177 us; the launch traced here: 176 us
  blocking collectives  170 us (96%)
  Pallas kernels  6.29 us (4%)
    all_to_all x12, blocking collectives, over(): return lax.all_to_all(value, names, 0, 0, tiled=True)  166 us
    pallas_call x15, Pallas kernels, call(): pl.pallas_call(body, out_shape=outs, in_specs=[whole(space)] * len(inputs...  6.29 us
    all_gather x2, blocking collectives, exchange(): both = lax.all_gather(sent, 'core', axis=0, tiled=True)  3.65 us

profile of v10, /device:TPU:24, one launch (start us, length us, event | category | flops | bytes accessed | tf_op | source)
XLA Modules:
  0.0 176.3 jit_solution(4385189701433346136)
XLA Ops:
  0.0 0.0 copy-start
  0.0 1.1 shard_map.46
  1.1 0.0 copy-start.1
  1.1 0.0 copy-start.2
  1.2 9.6 %all_to_all.60.received_ref = bf16[8,3,4,120]{3,2,1,0:T(4,128)(2,1)S(1)} all-to-all(bf16[8,3,4,120]{3,2,1,0:T(4,128)(2,1)S(1)} %get-tuple-element.15), channel_id=1, replica_groups=mesh['y1'=2,'y0'=2,'z3'=2,'z2'=2,'z1'=2,'z0'=2,'x'=4,'core'=2] {'x','core'}, dimensions={0} | all-to-all | bytes 46080 | tf_op jit(solution)/shard_map/all_to_all | solution.py:147
  10.8 0.0 copy-done
  10.8 0.4 shard_map.47
  11.2 10.0 %all_to_all.61.received_ref = f32[16,3,4,120]{3,2,1,0:T(4,128)S(1)} all-to-all(f32[16,3,4,120]{3,2,1,0:T(4,128)S(1)} %shard_map.47), channel_id=1, replica_groups=mesh['y1'=2,'y0'=2,'z3'=2,'z2'=2,'z1'=2,'z0'=2,'x'=4,'core'=2] {'z0','x'..., dimensions={0} | all-to-all | bytes 184320 | tf_op jit(solution)/shard_map/all_to_all | solution.py:147
  21.2 0.0 copy-done.1
  21.2 0.0 copy-done.2
  21.2 0.5 shard_map.48
  21.7 8.9 %all_to_all.62.received_ref = f32[16,3,4,120]{3,2,1,0:T(4,128)S(1)} all-to-all(f32[16,3,4,120]{3,2,1,0:T(4,128)S(1)} %get-tuple-element.17), channel_id=1, replica_groups=mesh['y1'=2,'y0'=2,'z3'=2,'z2'=2,'z1'=2,'z0'=2,'x'=4,'core'=2] {'z0','x'..., dimensions={0} | all-to-all | bytes 184320 | tf_op jit(solution)/shard_map/all_to_all | solution.py:147
  30.5 0.4 shard_map.49
  31.0 15.3 %all_to_all.63.received_ref = f32[32,3,4,120]{3,2,1,0:T(4,128)S(1)} all-to-all(f32[32,3,4,120]{3,2,1,0:T(4,128)S(1)} %shard_map.49), channel_id=1, replica_groups=mesh['y1'=2,'y0'=2,'z3'=2,'z2'=2,'z1'=2,'z0'=2,'x'=4,'core'=2] {'z0','x'..., dimensions={0} | all-to-all | bytes 368640 | tf_op jit(solution)/shard_map/all_to_all | solution.py:147
  46.3 0.5 shard_map.50
  46.7 11.6 %all_to_all.64.received_ref = bf16[32,3,4,120]{3,2,1,0:T(4,128)(2,1)S(1)} all-to-all(bf16[32,3,4,120]{3,2,1,0:T(4,128)(2,1)S(1)} %get-tuple-element.18), channel_id=1, replica_groups=mesh['y1'=2,'y0'=2,'z3'=2,'z2'=2,'z1'=2,'z0'=2,'x'=4,'core'=2] {'z0','x'..., dimensions={0} | all-to-all | bytes 184320 | tf_op jit(solution)/shard_map/all_to_all | solution.py:147
  58.3 0.4 shard_map.51
  58.8 23.3 %all_to_all.65.received_ref = bf16[32,3,4,120]{3,2,1,0:T(4,128)(2,1)S(1)} all-to-all(bf16[32,3,4,120]{3,2,1,0:T(4,128)(2,1)S(1)} %shard_map.51), channel_id=1, replica_groups=mesh['y1'=2,'y0'=2,'z3'=2,'z2'=2,'z1'=2,'z0'=2,'x'=4,'core'=2] {'z0','x'..., dimensions={0} | all-to-all | bytes 184320 | tf_op jit(solution)/shard_map/all_to_all | solution.py:147
  82.1 0.1 shard_map.52
  82.2 1.8 %all_gather.6.received_ref = bf16[8,3,4,120]{3,2,1,0:T(4,128)(2,1)S(1)} all-gather(bf16[4,3,4,120]{3,2,1,0:T(4,128)(2,1)S(1)} %get-tuple-element.19), channel_id=1, replica_groups=mesh['y1'=2,'y0'=2,'z3'=2,'z2'=2,'z1'=2,'z0'=2,'x'=4,'core'=2] {'core'}, dimensions={0}, use_global_device_ids=true | all-gather | bytes 34560 | tf_op jit(solution)/shard_map/all_gather | solution.py:248
  84.1 0.5 shard_map.53
  84.6 17.8 %all_to_all.66.received_ref = bf16[32,3,4,120]{3,2,1,0:T(4,128)(2,1)S(1)} all-to-all(bf16[32,3,4,120]{3,2,1,0:T(4,128)(2,1)S(1)} %shard_map.53), channel_id=1, replica_groups=mesh['y1'=2,'y0'=2,'z3'=2,'z2'=2,'z1'=2,'z0'=2,'x'=4,'core'=2] {'z0','x'..., dimensions={0} | all-to-all | bytes 184320 | tf_op jit(solution)/shard_map/all_to_all | solution.py:147
  102.4 1.8 %all_gather.7.received_ref = bf16[8,3,4,120]{3,2,1,0:T(4,128)(2,1)S(1)} all-gather(bf16[4,3,4,120]{3,2,1,0:T(4,128)(2,1)S(1)} %shard_map.54), channel_id=1, replica_groups=mesh['y1'=2,'y0'=2,'z3'=2,'z2'=2,'z1'=2,'z0'=2,'x'=4,'core'=2] {'core'}, dimensions={0}, use_global_device_ids=true | all-gather | bytes 34560 | tf_op jit(solution)/shard_map/all_gather | solution.py:248
  104.3 0.4 shard_map.55
  104.7 20.4 %all_to_all.67.received_ref = bf16[16,3,4,120]{3,2,1,0:T(4,128)(2,1)S(1)} all-to-all(bf16[16,3,4,120]{3,2,1,0:T(4,128)(2,1)S(1)} %shard_map.55), channel_id=1, replica_groups=mesh['y1'=2,'y0'=2,'z3'=2,'z2'=2,'z1'=2,'z0'=2,'x'=4,'core'=2] {'z1','z2..., dimensions={0} | all-to-all | bytes 92160 | tf_op jit(solution)/shard_map/all_to_all | solution.py:147
  125.1 0.1 shard_map.56
  125.2 7.8 %all_to_all.68.received_ref = bf16[8,3,4,120]{3,2,1,0:T(4,128)(2,1)S(1)} all-to-all(bf16[8,3,4,120]{3,2,1,0:T(4,128)(2,1)S(1)} %get-tuple-element.20), channel_id=1, replica_groups=mesh['y1'=2,'y0'=2,'z3'=2,'z2'=2,'z1'=2,'z0'=2,'x'=4,'core'=2] {'x','core'}, dimensions={0} | all-to-all | bytes 46080 | tf_op jit(solution)/shard_map/all_to_all | solution.py:147
  133.0 0.5 shard_map.57
  133.5 15.1 %all_to_all.69.received_ref = bf16[16,3,4,120]{3,2,1,0:T(4,128)(2,1)S(1)} all-to-all(bf16[16,3,4,120]{3,2,1,0:T(4,128)(2,1)S(1)} %shard_map.57), channel_id=1, replica_groups=mesh['y1'=2,'y0'=2,'z3'=2,'z2'=2,'z1'=2,'z0'=2,'x'=4,'core'=2] {'z1','z2..., dimensions={0} | all-to-all | bytes 92160 | tf_op jit(solution)/shard_map/all_to_all | solution.py:147
  148.7 7.8 %all_to_all.70.received_ref = bf16[8,3,4,120]{3,2,1,0:T(4,128)(2,1)S(1)} all-to-all(bf16[8,3,4,120]{3,2,1,0:T(4,128)(2,1)S(1)} %shard_map.58), channel_id=1, replica_groups=mesh['y1'=2,'y0'=2,'z3'=2,'z2'=2,'z1'=2,'z0'=2,'x'=4,'core'=2] {'x','core'}, dimensions={0} | all-to-all | bytes 46080 | tf_op jit(solution)/shard_map/all_to_all | solution.py:147
  156.4 0.6 shard_map.59
  157.0 18.6 %all_to_all.71.received_ref = bf16[32,3,4,120]{3,2,1,0:T(4,128)(2,1)S(1)} all-to-all(bf16[32,3,4,120]{3,2,1,0:T(4,128)(2,1)S(1)} %shard_map.59), channel_id=1, replica_groups=mesh['y1'=2,'y0'=2,'z3'=2,'z2'=2,'z1'=2,'z0'=2,'x'=4,'core'=2] {'z3','z2..., dimensions={0} | all-to-all | bytes 184320 | tf_op jit(solution)/shard_map/all_to_all | solution.py:147
  175.6 0.8 shard_map.60
  (2 shorter events, 0.1 us)
Async XLA Ops:
  0.0 10.8 %copy-start = (bf16[2,320,2480]{2,1,0:T(8,128)(2,1)S(1)}, bf16[2,320,2480]{2,1,0:T(8,128)(2,1)}, u32[]{:S(2)}) copy-start(bf16[2,320,2480]{2,1,0:T(8,128)(2,1)} %matrix.17) | copy-start | bytes 9523204
  1.1 20.1 %copy-start.1 = (bf16[2,320,1200]{2,1,0:T(8,128)(2,1)S(1)}, bf16[2,320,1200]{2,1,0:T(8,128)(2,1)}, u32[]{:S(2)}) copy-start(bf16[2,320,1200]{2,1,0:T(8,128)(2,1)} %matrix.16) | copy-start | bytes 4608004
  1.1 20.0 %copy-start.2 = (s32[1,30]{1,0:T(1,128)S(1)}, s32[1,30]{1,0:T(1,128)}, u32[]{:S(2)}) copy-start(s32[1,30]{1,0:T(1,128)} %mask.7) | copy-start | bytes 364
